TPU v7x, 32 devices: a whole 2x2x4 slice. The times are simulated.
32 devices in a mesh: parts: 2 (over y), space: 8 (over z, x), tm: 2 (over core).
Axes of the slice: x: 2, y: 2, z: 4, core: 2. Of those that a mesh axis runs over, the one named last changes fastest.
Arguments:
- eigvecs: bfloat16 [4, 2, 256, 3, 1728], P(('parts', 'tm'), None, None, None, 'space'), parts along dimension 0, may hold values from -1.25 to 1.25
- links: bfloat16 [4, 3, 3, 3, 2, 1728], P(('parts', 'tm'), None, None, None, None, 'space'), parts along dimension 0, may hold values from -2.5 to 2.5
- dirs: int32 [3], replicated, may hold values from 0 to 2, each once
- peram: bfloat16 [4, 2, 1024, 1024], P(('parts', 'tm'), None, 'space'), parts along dimension 0, may hold values from -0.25 to 0.25
Outputs:
- meson_blocks: bfloat16 [4, 3, 2, 1024, 1024], P(('parts', 'tm'), None, None, 'space'), parts along dimension 0
There are 2 independent parts, one for each index of `parts`. A program takes and returns all parts, laid end to end along the dimension named above; an argument that names none is the same for every part. Nothing has to cross between parts.
All inputs are finite; a program needn't handle non-finite values.
Results may differ from a plain program's by a relative error of at most 0.0061.
Values may be sent and summed in bfloat16 or wider, within the bound.
No kernel may reach another device: no remote copies, remote signals or barrier semaphores. Data moves between devices by JAX's collectives and lax.ppermute only.
A program may use at most 64 MiB of HBM per device.

v0:
```python
import jax
import jax.numpy as jnp
from jax import lax
from jax.sharding import PartitionSpec as P

K = 256
SPIN = 4
LX = 9
LZ = 24


def from_behind(block, axis, distance):
    devices = range(lax.axis_size(axis))
    route = [((i - distance) % len(devices), i) for i in devices]
    return lax.ppermute(block, axis, route)


def link_apply(link_mat, values_in, adjoint):
    real_rows = []
    imag_rows = []
    for out_row in range(3):
        real_sum = jnp.zeros(values_in.shape[1:2] + values_in.shape[3:], jnp.float32)
        imag_sum = jnp.zeros(values_in.shape[1:2] + values_in.shape[3:], jnp.float32)
        for in_col in range(3):
            if adjoint:
                link_entry = link_mat[in_col, out_row]
                conj_sign = -1.0
            else:
                link_entry = link_mat[out_row, in_col]
                conj_sign = 1.0
            link_real = link_entry[0].astype(jnp.float32)[None]
            link_imag = (conj_sign * link_entry[1].astype(jnp.float32))[None]
            vec_real = values_in[0, :, in_col].astype(jnp.float32)
            vec_imag = values_in[1, :, in_col].astype(jnp.float32)
            real_sum = real_sum + link_real * vec_real - link_imag * vec_imag
            imag_sum = imag_sum + link_real * vec_imag + link_imag * vec_real
        real_rows.append(real_sum)
        imag_rows.append(imag_sum)
    return jnp.stack([jnp.stack(real_rows, axis=1), jnp.stack(imag_rows, axis=1)])


def contract(left, right):
    return lax.dot_general(
        left, right, (((1,), (1,)), ((), ())), preferred_element_type=jnp.float32
    )


def elemental(eigen_field, derivative):
    vectors = eigen_field.shape[1]
    vec_real = eigen_field[0].reshape(vectors, -1)
    vec_imag = eigen_field[1].reshape(vectors, -1)
    der_real = derivative[0].reshape(vectors, -1)
    der_imag = derivative[1].reshape(vectors, -1)
    return jnp.stack(
        [
            contract(vec_real, der_real) + contract(vec_imag, der_imag),
            contract(vec_real, der_imag) - contract(vec_imag, der_real),
        ]
    )


def lattice(values):
    return values.reshape(values.shape[:-1] + (values.shape[-1] // (LX * LZ), LX, LZ))


def on_device(eigvecs, links, dirs, peram):
    eig_lat = lattice(eigvecs)
    link_lat = lattice(links)
    slab_rows = eig_lat.shape[4]
    back_y = jnp.stack([link_apply(link_lat[0, 1], eig_lat[0], True).astype(jnp.bfloat16)])
    y_ahead = from_behind(eig_lat[:, :, :, :, 0], "space", -1)
    y_behind = from_behind(back_y[:, :, :, :, slab_rows - 1], "space", 1)
    choose = dirs[:, None] == jnp.arange(3, dtype=jnp.int32)[None, :]
    position = 0
    eigen_field = eig_lat[position]
    link_set = link_lat[position]
    elementals = []
    for direction in range(3):
        if direction == 0:
            ahead_field = jnp.roll(eigen_field, -1, axis=4)
            back_term = link_apply(link_set[0], eigen_field, True).astype(jnp.bfloat16)
            behind = jnp.roll(back_term, 1, axis=4)
        elif direction == 1:
            ahead_field = jnp.concatenate(
                [eigen_field[:, :, :, 1:], y_ahead[position][:, :, :, None]], axis=3
            )
            behind = jnp.concatenate(
                [y_behind[position][:, :, :, None], back_y[position][:, :, :, :-1]], axis=3
            )
        else:
            ahead_field = jnp.roll(eigen_field, -1, axis=5)
            back_term = link_apply(link_set[2], eigen_field, True).astype(jnp.bfloat16)
            behind = jnp.roll(back_term, 1, axis=5)
        derivative = (
            link_apply(link_set[direction], ahead_field, False) - behind.astype(jnp.float32)
        ).astype(jnp.bfloat16)
        elementals.append(elemental(eigen_field, derivative))
    elementals = jnp.stack(elementals)
    picked_all = [jnp.sum(jnp.where(choose[:, :, None, None, None], elementals[None], 0.0), axis=1)]
    stacked = jnp.stack(picked_all)
    elem_low = lax.psum(stacked, "space").astype(jnp.bfloat16)
    blocks = from_behind(peram, "tm", -1)
    columns = blocks.shape[2]
    position = 0
    elem_real = elem_low[position, :, 0]
    elem_imag = elem_low[position, :, 1]
    peram_real = blocks[position, 0].reshape(columns, K, SPIN)
    peram_imag = blocks[position, 1].reshape(columns, K, SPIN)
    out_real = jnp.einsum(
        "jkl,cls->jcks", elem_real, peram_real, preferred_element_type=jnp.float32
    ) - jnp.einsum("jkl,cls->jcks", elem_imag, peram_imag, preferred_element_type=jnp.float32)
    out_imag = jnp.einsum(
        "jkl,cls->jcks", elem_real, peram_imag, preferred_element_type=jnp.float32
    ) + jnp.einsum("jkl,cls->jcks", elem_imag, peram_real, preferred_element_type=jnp.float32)
    combined = jnp.stack([out_real, out_imag], axis=1)
    results = [combined.reshape(combined.shape[0], 2, columns, K * SPIN).astype(jnp.bfloat16)]
    return jnp.stack(results)


def solution(mesh):
    placed = (
        P(("parts", "tm"), None, None, None, "space"),
        P(("parts", "tm"), None, None, None, None, "space"),
        P(),
        P(("parts", "tm"), None, "space", None),
    )
    return jax.shard_map(
        on_device,
        mesh=mesh,
        in_specs=placed,
        out_specs=P(("parts", "tm"), None, None, "space", None),
        check_vma=False,
    )
```

profile of v0, /device:TPU:0, one launch (start us, length us, event | category | flops | bytes accessed | tf_op | source)
XLA Modules:
  0.0 128.3 jit_solution(4704577270389625453)
XLA Ops:
  0.0 1.0 reshape.4464
  1.1 1.5 %fusion.160 = (bf16[256,1,1,9,24]{0,4,3,1,2:T(8,128)(2,1)S(1)}, bf16[256,1,1,9,24]{0,4,3,1,2:T(8,128)(2,1)S(1)}) fusion(f32[9,24]{1,0:T(8,128)S(1)} %get-tuple-element.98, f32[9,24]{1,0:T(8,128)S(1)} %get-tuple-element.89, f32[9,24]{1,0:T(8,128)S(1)} %get-tuple-element.99, f32[9,24]{1,0:T(8,128)S(1)} %get-tuple-element.90, ...), kind=kLoop, calls=%fused_computation.422 | loop fusion | flops 1658880 | bytes 889920 | tf_op jit(solution)/shard_map/convert.111
  3.3 0.9 pad_maximum_fusion.7
  4.2 3.0 %collective-permute-start.1 = (bf16[1,2,256,3,9,24]{2,5,4,3,1,0:T(8,128)(2,1)}, bf16[1,2,256,3,9,24]{2,5,4,3,1,0:T(8,128)(2,1)}, u32[]{:S(2)}, u32[]{:S(2)}) collective-permute-start(bf16[1,2,256,3,9,24]{2,5,4,3,1,0:T(8,128)(2,1)} %pad_maximum_fusion.7), channel_id=1, source_target_pairs={{14,0},{0,2},{2,4},{4,6},{6,8},{8,10},{10,12},{12,14},{15,1},{1,3}... | collective-permute-start | bytes 1990664 | tf_op jit(solution)/shard_map/ppermute | solution.py:15
  7.2 3.0 %collective-permute-start = (bf16[1,2,256,3,9,24]{2,5,4,3,1,0:T(8,128)(2,1)S(1)}, bf16[1,2,256,3,9,24]{2,5,4,3,1,0:T(8,128)(2,1)S(1)}, u32[]{:S(2)}, u32[]{:S(2)}) collective-permute-start(bf16[1,2,256,3,9,24]{2,5,4,3,1,0:T(8,128)(2,1)S(1)} %bitcast.1013), channel_id=1, source_target_pairs={{2,0},{4,2},{6,4},{8,6},{10,8},{12,10},{14,12},{0,14},{3,1},{5,3},... | collective-permute-start | bytes 1990664 | tf_op jit(solution)/shard_map/ppermute | solution.py:15
  10.2 1.0 copy.140
  11.2 0.6 fusion.315
  12.1 0.6 fusion.296
  12.7 0.6 fusion.295
  13.3 0.6 broadcast_multiply_fusion.17
  14.7 0.6 broadcast_multiply_fusion.8
  16.5 0.9 fusion.25
  17.5 0.9 fusion.30
  18.4 0.9 fusion.27
  19.4 0.9 fusion.35
  28.2 0.8 maximum_bitcast_fusion.6
  29.0 0.8 maximum_bitcast_fusion.8
  29.9 1.1 fusion.314
  31.2 0.9 copy.141
  32.0 5.7 %collective-permute-done = bf16[1,2,256,3,9,24]{2,5,4,3,1,0:T(8,128)(2,1)S(1)} collective-permute-done((bf16[1,2,256,3,9,24]{2,5,4,3,1,0:T(8,128)(2,1)S(1)}, bf16[1,2,256,3,9,24]{2,5,4,3,1,0:T(8,128)(2,1)S(1)}, u32[]{:S(2)}, u32[]{:S(2)}) %collective-permute-start) | collective-permute-done | bytes 663584 | tf_op jit(solution)/shard_map/ppermute | solution.py:15
  38.8 1.3 %fusion.1 = bf16[2,256,3,1,9,24]{1,5,4,2,0,3:T(8,128)(2,1)S(1)} fusion(f32[1,256,3,1,9,24]{1,5,4,2,0,3:T(8,128)S(1)} %get-tuple-element.151, f32[1,256,3,1,9,24]{1,5,4,2,0,3:T(8,128)S(1)} %get-tuple-element.150, bf16[1,2,256,3,9,24]{2,5,4,3,1,0:T(8,128)(2,1)} %collective-permute-done.1), kind=kLoop, calls=%fused_computation.14 | loop fusion | flops 1327104 | bytes 2654208 | tf_op jit(solution)/shard_map/convert_element_type | solution.py:96
  43.4 79.8 %all-reduce.1 = bf16[1,3,2,256,256]{4,3,1,2,0:T(8,128)(2,1)S(1)} all-reduce(f32[1,3,2,256,256]{4,3,1,2,0:T(8,128)S(1)} %bitcast.1036), channel_id=1, replica_groups=mesh['parts'=2,'space'=8,'tm'=2] {'space'}, use_global_device_ids=true, to_apply=%region_1.2 | all-reduce | flops 393216 | bytes 2359296 | tf_op jit(solution)/shard_map/psum | solution.py:101
  124.9 0.6 copy.143
  126.7 1.6 %copy.147 = bf16[1,3,2,128,1024]{4,3,2,1,0:T(8,128)(2,1)} copy(bf16[1,3,2,128,1024]{3,4,1,2,0:T(8,128)(2,1)S(1)} %pad_maximum_fusion.1) | data formatting | bytes 3145728 | tf_op jit(solution)/shard_map/stack | solution.py:115
  (161 shorter events, 17.3 us)
Async XLA Ops:
  0.0 2.6 %copy-start = (bf16[1,2,256,3,216]{2,4,3,1,0:T(8,128)(2,1)S(1)}, bf16[1,2,256,3,216]{2,4,3,1,0:T(8,128)(2,1)}, u32[]{:S(2)}) copy-start(bf16[1,2,256,3,216]{2,4,3,1,0:T(8,128)(2,1)} %param.4) | copy-start | bytes 1990660
  2.9 7.3 %copy-start.8 = (bf16[1,2,128,1024]{3,2,1,0:T(8,128)(2,1)S(1)}, bf16[1,2,128,1024]{3,2,1,0:T(8,128)(2,1)}, u32[]{:S(2)}) copy-start(bf16[1,2,128,1024]{3,2,1,0:T(8,128)(2,1)} %param.7) | copy-start | bytes 1572868
  3.2 8.0 %copy-start.9 = (bf16[1,3,3,3,2,216]{5,4,3,2,1,0:T(2,128)(2,1)S(1)}, bf16[1,3,3,3,2,216]{5,4,3,2,1,0:T(2,128)(2,1)}, u32[]{:S(2)}) copy-start(bf16[1,3,3,3,2,216]{5,4,3,2,1,0:T(2,128)(2,1)} %param.5) | copy-start | bytes 69988
  4.2 34.6 %collective-permute-start.1 = (bf16[1,2,256,3,9,24]{2,5,4,3,1,0:T(8,128)(2,1)}, bf16[1,2,256,3,9,24]{2,5,4,3,1,0:T(8,128)(2,1)}, u32[]{:S(2)}, u32[]{:S(2)}) collective-permute-start(bf16[1,2,256,3,9,24]{2,5,4,3,1,0:T(8,128)(2,1)} %pad_maximum_fusion.7), channel_id=1, source_target_pairs={{14,0},{0,2},{2,4},{4,6},{6,8},{8,10},{10,12},{12,14},{15,1},{1,3}... | collective-permute-start | bytes 1990664 | tf_op jit(solution)/shard_map/ppermute | solution.py:15
  7.2 30.6 %collective-permute-start = (bf16[1,2,256,3,9,24]{2,5,4,3,1,0:T(8,128)(2,1)S(1)}, bf16[1,2,256,3,9,24]{2,5,4,3,1,0:T(8,128)(2,1)S(1)}, u32[]{:S(2)}, u32[]{:S(2)}) collective-permute-start(bf16[1,2,256,3,9,24]{2,5,4,3,1,0:T(8,128)(2,1)S(1)} %bitcast.1013), channel_id=1, source_target_pairs={{2,0},{4,2},{6,4},{8,6},{10,8},{12,10},{14,12},{0,14},{3,1},{5,3},... | collective-permute-start | bytes 1990664 | tf_op jit(solution)/shard_map/ppermute | solution.py:15
  11.2 18.7 %collective-permute-start.2 = (bf16[1,2,128,1024]{2,3,1,0:T(8,128)(2,1)}, bf16[1,2,128,1024]{2,3,1,0:T(8,128)(2,1)}, u32[]{:S(2)}, u32[]{:S(2)}) collective-permute-start(bf16[1,2,128,1024]{2,3,1,0:T(8,128)(2,1)} %copy.140), channel_id=1, source_target_pairs={{1,0},{0,1},{3,2},{2,3},{5,4},{4,5},{7,6},{6,7},{9,8},{8,9},{11,10... | collective-permute-start | bytes 1572872 | tf_op jit(solution)/shard_map/ppermute | solution.py:15
  17.5 2.8 %copy-start.10 = (f32[9,24]{1,0:T(8,128)S(1)}, f32[9,24]{1,0:T(8,128)}, u32[]{:S(2)}) copy-start(f32[9,24]{1,0:T(8,128)} %get-tuple-element.64) | copy-start | bytes 2596
  17.5 2.8 %copy-start.14 = (f32[9,24]{1,0:T(8,128)S(1)}, f32[9,24]{1,0:T(8,128)}, u32[]{:S(2)}) copy-start(f32[9,24]{1,0:T(8,128)} %get-tuple-element.68) | copy-start | bytes 2596
  17.5 2.8 %copy-start.39 = (f32[9,24]{1,0:T(8,128)S(1)}, f32[9,24]{1,0:T(8,128)}, u32[]{:S(2)}) copy-start(f32[9,24]{1,0:T(8,128)} %get-tuple-element.56) | copy-start | bytes 2596
  17.5 2.8 %copy-start.40 = (f32[9,24]{1,0:T(8,128)S(1)}, f32[9,24]{1,0:T(8,128)}, u32[]{:S(2)}) copy-start(f32[9,24]{1,0:T(8,128)} %get-tuple-element.58) | copy-start | bytes 2596
  17.5 2.8 %copy-start.41 = (f32[9,24]{1,0:T(8,128)S(1)}, f32[9,24]{1,0:T(8,128)}, u32[]{:S(2)}) copy-start(f32[9,24]{1,0:T(8,128)} %get-tuple-element.61) | copy-start | bytes 2596
  18.4 2.3 %copy-start.12 = (f32[9,24]{1,0:T(8,128)S(1)}, f32[9,24]{1,0:T(8,128)}, u32[]{:S(2)}) copy-start(f32[9,24]{1,0:T(8,128)} %get-tuple-element.66) | copy-start | bytes 2596
  18.4 2.3 %copy-start.13 = (f32[9,24]{1,0:T(8,128)S(1)}, f32[9,24]{1,0:T(8,128)}, u32[]{:S(2)}) copy-start(f32[9,24]{1,0:T(8,128)} %get-tuple-element.67) | copy-start | bytes 2596
  18.4 2.3 %copy-start.36 = (f32[9,24]{1,0:T(8,128)S(1)}, f32[9,24]{1,0:T(8,128)}, u32[]{:S(2)}) copy-start(f32[9,24]{1,0:T(8,128)} %get-tuple-element.57) | copy-start | bytes 2596
  18.4 2.3 %copy-start.37 = (f32[9,24]{1,0:T(8,128)S(1)}, f32[9,24]{1,0:T(8,128)}, u32[]{:S(2)}) copy-start(f32[9,24]{1,0:T(8,128)} %get-tuple-element.60) | copy-start | bytes 2596
  18.4 2.3 %copy-start.38 = (f32[9,24]{1,0:T(8,128)S(1)}, f32[9,24]{1,0:T(8,128)}, u32[]{:S(2)}) copy-start(f32[9,24]{1,0:T(8,128)} %get-tuple-element.63) | copy-start | bytes 2596
  23.6 1.2 copy-start.23
  24.0 1.2 copy-start.17
  24.0 1.2 copy-start.18
  24.0 1.2 copy-start.19
  24.3 1.2 copy-start.20
  24.3 1.2 copy-start.21
  24.3 1.2 copy-start.22
  27.8 2.0 %copy-start.44 = (s32[3]{0:T(128)S(1)}, s32[3]{0:T(128)}, u32[]{:S(2)}) copy-start(s32[3]{0:T(128)} %param.6) | copy-start | bytes 40
  (24 other events, 25.3 us)
where the time goes:
time: 129 us; the launch traced here: 128 us
  blocking collectives  79.8 us (62%)
  other arithmetic  19.6 us (15%)
  local copies, waits for them, and re-layouts  10.9 us (8%)
  starting transfers between devices  6.01 us (5%)
  waiting for transfers between devices  5.73 us (4%)
  matrix products  5.24 us (4%)
    psum x1, blocking collectives, on_device(): elem_low = lax.psum(stacked, 'space').astype(jnp.bfloat16)  79.8 us
    ppermute x3, starting transfers between devices, from_behind(): return lax.ppermute(block, axis, route)  6.01 us
    ppermute x3, waiting for transfers between devices, from_behind(): return lax.ppermute(block, axis, route)  5.73 us
    another operation x9, other arithmetic  3.94 us
    sub x8, other arithmetic, link_apply(): real_sum = real_sum + link_real * vec_real - link_imag * vec_imag  3.79 us
    dot_general x12, matrix products, contract(): lax.dot_general(left, right, (((1,), (1,)), ((), ())), preferred_element_...  3.67 us
    unnamed x91, local copies, waits for them, and re-layouts  2.59 us
  transfers between devices with their start and end apart: 3, of which 1 were waited for; matrix products, arithmetic and copies ran while one was open for 17% of the time, Pallas kernels for 0%

commit v1 on v0

v1 whole, which is shorter than its diff:
```python
import functools

import jax
import jax.numpy as jnp
from jax import lax
from jax.experimental import pallas as pl
from jax.experimental.pallas import tpu as pltpu
from jax.sharding import PartitionSpec as P

SPIN = 4
LX = 9
LZ = 24
F32 = jnp.float32
BF16 = jnp.bfloat16
VMEM = pl.BlockSpec(memory_space=pltpu.VMEM)


def half_rows(sites):
    return 8 * ((sites + 15) // 16)


def padded(count):
    return 8 * ((count + 7) // 8)


def identity(size):
    rows = lax.broadcasted_iota(jnp.int32, (size, size), 0)
    cols = lax.broadcasted_iota(jnp.int32, (size, size), 1)
    return jnp.where(rows == cols, 1.0, 0.0).astype(BF16)


def dot(left, right, left_dim, right_dim):
    return lax.dot_general(
        left, right, (((left_dim,), (right_dim,)), ((), ())), preferred_element_type=F32
    )


def adjoint_product(columns, base, vec):
    real_rows, imag_rows = [], []
    for out in range(3):
        real_sum = imag_sum = None
        for inner in range(3):
            at = base + (inner * 3 + out) * 2
            link_real = columns[:, at : at + 1]
            link_imag = columns[:, at + 1 : at + 2]
            real = link_real * vec[inner] + link_imag * vec[3 + inner]
            imag = link_real * vec[3 + inner] - link_imag * vec[inner]
            real_sum = real if real_sum is None else real_sum + real
            imag_sum = imag if imag_sum is None else imag_sum + imag
        real_rows.append(real_sum)
        imag_rows.append(imag_sum)
    return real_rows + imag_rows


def packed_elemental(w_real, w_imag, v_real, v_imag):
    real = dot(w_real, v_real, 0, 0) + dot(w_imag, v_imag, 0, 0)
    imag = dot(w_real, v_imag, 0, 0) - dot(w_imag, v_real, 0, 0)
    return (real + imag) + jnp.transpose(imag - real)


def prepare_kernel(sites, v_ref, u_ref, across_ref, along_ref):
    half = half_rows(sites)
    overlap = 2 * half - sites
    vectors = v_ref.shape[1]
    parity = lax.rem(lax.axis_index("space"), 2)
    entries = u_ref.shape[0]

    def fill(ref, upper):
        first = sites - half if upper else 0
        for comp in range(6):
            ref[pl.ds(comp * half, half), :] = v_ref[pl.ds(comp * sites + first, half), :]
        links = u_ref[:, first : first + half].astype(F32)
        if upper and overlap:
            lane = lax.broadcasted_iota(jnp.int32, links.shape, 1)
            links = jnp.where(lane < overlap, 0.0, links)
        rows = ref.shape[0] - 6 * half
        block = jnp.concatenate(
            [
                jnp.concatenate([links, jnp.zeros((rows - entries, half), F32)], axis=0),
                jnp.zeros((rows, vectors - half), F32),
            ],
            axis=1,
        )
        ref[pl.ds(6 * half, rows), :] = block.astype(BF16)

    @pl.when(parity == 0)
    def _():
        fill(across_ref, True)
        fill(along_ref, False)

    @pl.when(parity == 1)
    def _():
        fill(across_ref, False)
        fill(along_ref, True)


def front_kernel(sites, v_ref, u_ref, o_ref, w_ref):
    planes = sites // LZ
    vectors = v_ref.shape[1]
    columns = dot(identity(sites), u_ref[...], 1, 1)
    for plane in range(planes):
        slab, along = plane // LX, plane % LX
        start = plane * LZ
        vec = [v_ref[pl.ds(comp * sites + start, LZ), :].astype(F32) for comp in range(6)]
        here = columns[start : start + LZ, :]
        ahead = (slab * LX + (along + 1) % LX) * LZ
        for comp, value in enumerate(adjoint_product(here, 0, vec)):
            w_ref[0, pl.ds(comp * sites + ahead, LZ), :] = value
        for comp, value in enumerate(adjoint_product(here, 18, vec)):
            w_ref[1, pl.ds(comp * sites + start, LZ), :] = pltpu.roll(value, 1, 0)
    real = pl.ds(0, 3 * sites)
    imag = pl.ds(3 * sites, 3 * sites)
    for index in range(2):
        packed = packed_elemental(
            w_ref[index, real, :].astype(BF16),
            w_ref[index, imag, :].astype(BF16),
            v_ref[real, :],
            v_ref[imag, :],
        )
        o_ref[pl.ds(index * vectors, vectors), :] = packed.astype(BF16)


def middle_kernel(half, own_ref, across_ref, along_ref, o_ref, w_ref):
    even = lax.rem(lax.axis_index("space"), 2) == 0
    first = jnp.where(even, own_ref[...], along_ref[...])
    last = jnp.where(even, along_ref[...], own_ref[...])
    middle = across_ref[...]
    ident = identity(half)
    for index, field in enumerate((first, middle)):
        columns = dot(ident, field[6 * half :, :half], 1, 1)
        vec = [field[comp * half : (comp + 1) * half, :].astype(F32) for comp in range(6)]
        for comp, value in enumerate(adjoint_product(columns, 0, vec)):
            part, inner = comp // 3, comp % 3
            w_ref[part, pl.ds((index * 3 + inner) * half, half), :] = value
    v_real = jnp.concatenate([middle[: 3 * half], last[: 3 * half]], axis=0)
    v_imag = jnp.concatenate([middle[3 * half : 6 * half], last[3 * half : 6 * half]], axis=0)
    packed = packed_elemental(w_ref[0].astype(BF16), w_ref[1].astype(BF16), v_real, v_imag)
    o_ref[...] = packed.astype(BF16)


def spread(size):
    rows = lax.broadcasted_iota(jnp.int32, (SPIN * size, SPIN * size), 0)
    cols = lax.broadcasted_iota(jnp.int32, (SPIN * size, SPIN * size), 1)
    target = (rows % size) * SPIN + rows // size
    return jnp.where(cols == target, 1.0, 0.0).astype(BF16)


def spins_kernel(p_ref, o_ref, s_ref):
    columns, wide = p_ref.shape[1], p_ref.shape[2]
    vectors = wide // SPIN
    block = 128
    table = spread(block)
    s_ref[...] = table
    for part in range(2):
        for chunk in range(vectors // block):
            piece = p_ref[part, :, pl.ds(chunk * block * SPIN, block * SPIN)]
            apart = dot(piece, table, 1, 1).astype(BF16)
            for spin in range(SPIN):
                o_ref[
                    pl.ds(spin * columns, columns),
                    pl.ds(part * vectors + chunk * block, block),
                ] = apart[:, spin * block : (spin + 1) * block]


def last_kernel(places_ref, m_ref, p_ref, s_ref, *rest):
    o_ref = rest[-1]
    columns = o_ref.shape[2]
    vectors = m_ref.shape[1]
    block = s_ref.shape[0] // SPIN
    packed = m_ref[...].astype(F32)
    turned = jnp.transpose(packed)
    real = (0.5 * (turned - packed)).astype(BF16)
    imag = (0.5 * (packed + turned)).astype(BF16)
    minus = -imag
    right = jnp.concatenate(
        [jnp.concatenate([real, imag], axis=1), jnp.concatenate([minus, real], axis=1)], axis=0
    )
    product = dot(p_ref[...], right, 1, 0).astype(BF16)
    for part in range(2):
        for chunk in range(vectors // block):
            at = part * vectors + chunk * block
            piece = jnp.concatenate(
                [product[spin * columns : (spin + 1) * columns, at : at + block] for spin in range(SPIN)],
                axis=1,
            )
            o_ref[0, part, :, pl.ds(chunk * block * SPIN, block * SPIN)] = dot(
                piece, s_ref[...], 1, 0
            ).astype(BF16)


def last_call(places, packed, spins, table, shape, result=None):
    vectors = packed.shape[1]
    count = packed.shape[0] // vectors
    specs = [
        pl.BlockSpec((vectors, vectors), lambda i, at: (i, 0)),
        pl.BlockSpec(spins.shape, lambda i, at: (0, 0)),
        pl.BlockSpec(table.shape, lambda i, at: (0, 0)),
    ]
    args = [places, packed, spins, table]
    aliases = {}
    if result is not None:
        specs.append(pl.BlockSpec(memory_space=pl.ANY))
        args.append(result)
        aliases = {4: 0}
    return pl.pallas_call(
        last_kernel,
        grid_spec=pltpu.PrefetchScalarGridSpec(
            num_scalar_prefetch=1,
            grid=(count,),
            in_specs=specs,
            out_specs=pl.BlockSpec((1,) + shape[1:], lambda i, at: (at[i], 0, 0, 0)),
        ),
        out_shape=jax.ShapeDtypeStruct(shape, BF16),
        input_output_aliases=aliases,
        cost_estimate=pl.CostEstimate(flops=count * 800_000_000, bytes_accessed=count * 1_000_000, transcendentals=0),
    )(*args)


def sum_over_space(partial, ranks):
    rows, width = partial.shape
    pieces = lax.all_to_all(
        partial.reshape(ranks, rows // ranks, width), "space", 0, 0, tiled=True
    )
    total = jnp.sum(pieces.astype(F32), axis=0).astype(BF16)
    whole = lax.all_to_all(
        jnp.broadcast_to(total[None], (ranks,) + total.shape), "space", 0, 0, tiled=True
    )
    return whole.reshape(rows, width)


def on_device(eigvecs, links, dirs, peram):
    ranks = lax.axis_size("space")
    vectors, sites = eigvecs.shape[2], eigvecs.shape[4]
    assert sites == LX * LZ and ranks % 2 == 0
    field = jnp.transpose(eigvecs[0], (0, 2, 3, 1)).reshape(6 * sites, vectors)
    link_rows = links[0].reshape(54, sites)
    half = half_rows(sites)
    rows = 6 * half + padded(18)

    payload = jax.ShapeDtypeStruct((rows, vectors), BF16)
    across, along = pl.pallas_call(
        functools.partial(prepare_kernel, sites),
        out_shape=(payload, payload),
        in_specs=[VMEM] * 2,
        out_specs=(VMEM, VMEM),
    )(field, link_rows[18:36])
    from_across = lax.ppermute(across, "space", [(i, i ^ 1) for i in range(ranks)])
    from_along = lax.ppermute(
        along,
        "space",
        [((i + 2) % ranks if i % 2 == 0 else (i - 2) % ranks, i) for i in range(ranks)],
    )
    partner = lax.ppermute(peram[0], "tm", [((i + 1) % 2, i) for i in range(2)])

    flat = pl.pallas_call(
        functools.partial(front_kernel, sites),
        out_shape=jax.ShapeDtypeStruct((2 * vectors, vectors), BF16),
        in_specs=[VMEM] * 2,
        out_specs=VMEM,
        scratch_shapes=[pltpu.VMEM((2, 6 * sites, vectors), F32)],
        cost_estimate=pl.CostEstimate(flops=700_000_000, bytes_accessed=8_000_000, transcendentals=0),
    )(field, jnp.concatenate([link_rows[:18], link_rows[36:]]))
    columns = partner.shape[1]
    spins, table = pl.pallas_call(
        spins_kernel,
        out_shape=(
            jax.ShapeDtypeStruct((SPIN * columns, 2 * vectors), BF16),
            jax.ShapeDtypeStruct((SPIN * 128, SPIN * 128), BF16),
        ),
        in_specs=[VMEM],
        out_specs=(VMEM, VMEM),
        cost_estimate=pl.CostEstimate(flops=500_000_000, bytes_accessed=2_000_000, transcendentals=0),
    )(partner)
    whole_flat = sum_over_space(flat, ranks)
    upright = pl.pallas_call(
        functools.partial(middle_kernel, half),
        out_shape=jax.ShapeDtypeStruct((vectors, vectors), BF16),
        in_specs=[VMEM] * 3,
        out_specs=VMEM,
        scratch_shapes=[pltpu.VMEM((2, 6 * half, vectors), F32)],
        cost_estimate=pl.CostEstimate(flops=400_000_000, bytes_accessed=4_000_000, transcendentals=0),
    )(along, from_across, from_along)
    whole_upright = sum_over_space(upright, ranks)

    count = dirs.shape[0]
    order = jnp.arange(count, dtype=jnp.int32)
    places = jnp.sum(jnp.where(dirs[None, :] == order[:, None], order[None, :], 0), axis=1)
    shape = (count, 2, columns, SPIN * vectors)
    result = last_call(jnp.stack([places[0], places[2]]), whole_flat, spins, table, shape)
    result = last_call(places[1:2], whole_upright, spins, table, shape, result)
    return result[None]


def solution(mesh):
    placed = (
        P(("parts", "tm"), None, None, None, "space"),
        P(("parts", "tm"), None, None, None, None, "space"),
        P(),
        P(("parts", "tm"), None, "space", None),
    )
    return jax.shard_map(
        on_device,
        mesh=mesh,
        in_specs=placed,
        out_specs=P(("parts", "tm"), None, None, "space", None),
        check_vma=False,
    )
```

time: 129 us -> 77.2 us (0.60)
  blocking collectives: 79.8 us -> 0 us
  Pallas kernels: 0 us -> 21.6 us
  starting transfers between devices: 6.01 us -> 24.4 us
  other arithmetic: 19.6 us -> 2.63 us
  waiting for transfers between devices: 5.73 us -> 22.1 us
  local copies, waits for them, and re-layouts: 10.9 us -> 5.63 us
  matrix products: 5.24 us -> 0 us
    psum x1 -> x0, blocking collectives: 79.8 us -> none  [on_device(): elem_low = lax.psum(stacked, 'space').astype(jnp.bfloat16)]
    pallas_call x0 -> x6, Pallas kernels: none -> 21.6 us  [the longest x2 8.14 us: last_call(): pl.pallas_call(last_kernel, grid_spec=pltpu.PrefetchScalarGridSpec(num_sc...]
    all_to_all x0 -> x4, starting transfers between devices: none -> 19.1 us  [the longest x2 12.3 us: sum_over_space(): lax.all_to_all(partial.reshape(ranks, rows // ranks, width), 'space', 0,...]
    all_to_all x0 -> x4, waiting for transfers between devices: none -> 14.6 us  [the longest x2 7.3 us: sum_over_space(): lax.all_to_all(partial.reshape(ranks, rows // ranks, width), 'space', 0,...]
    another operation x22 -> x1, other arithmetic: 7.29 us -> 1.84 us  [on_device(): jnp.stack([places[0], places[2]])]
    dot_general x16 -> x0, matrix products: 5.24 us -> none  [the longest x12 3.67 us: contract(): lax.dot_general(left, right, (((1,), (1,)), ((), ())), preferred_element_...]
    convert_element_type x9 -> x0, other arithmetic: 3.86 us -> none  [the longest x3 1.95 us: on_device(): derivative = (link_apply(link_set[direction], ahead_field, False) - behin...]
    sub x8 -> x0, other arithmetic: 3.79 us -> none  [link_apply(): real_sum = real_sum + link_real * vec_real - link_imag * vec_imag]
  transfers between devices with their start and end apart: 3 -> 7, of which waited for: 1 -> 4; matrix products, arithmetic and copies ran while one was open for 17% -> 5% of each run, Pallas kernels for 0% -> 17%
where the time goes in v1:
time: 77.2 us; the launch traced here: 76.4 us
  starting transfers between devices  24.4 us (32%)
  waiting for transfers between devices  22.1 us (29%)
  Pallas kernels  21.6 us (28%)
  local copies, waits for them, and re-layouts  5.63 us (7%)
  other arithmetic  2.63 us (3%)
    all_to_all x2, starting transfers between devices, sum_over_space(): lax.all_to_all(partial.reshape(ranks, rows // ranks, width), 'space', 0,...  12.3 us
    pallas_call x2, Pallas kernels, last_call(): pl.pallas_call(last_kernel, grid_spec=pltpu.PrefetchScalarGridSpec(num_sc...  8.14 us
    all_to_all x2, waiting for transfers between devices, sum_over_space(): lax.all_to_all(partial.reshape(ranks, rows // ranks, width), 'space', 0,...  7.3 us
    all_to_all x2, waiting for transfers between devices, sum_over_space(): lax.all_to_all(jnp.broadcast_to(total[None], (ranks,) + total.shape), 'sp...  7.3 us
    all_to_all x2, starting transfers between devices, sum_over_space(): lax.all_to_all(jnp.broadcast_to(total[None], (ranks,) + total.shape), 'sp...  6.78 us
    ppermute x1, waiting for transfers between devices, on_device(): lax.ppermute(across, 'space', [(i, i ^ 1) for i in range(ranks)])  6.11 us
    pallas_call x1, Pallas kernels, on_device(): pl.pallas_call(functools.partial(front_kernel, sites), out_shape=jax.Shap...  4.96 us
    pallas_call x1, Pallas kernels, on_device(): pl.pallas_call(functools.partial(middle_kernel, half), out_shape=jax.Shap...  3.73 us
  transfers between devices with their start and end apart: 7, of which 4 were waited for; matrix products, arithmetic and copies ran while one was open for 5% of the time, Pallas kernels for 17%

profile of v1, /device:TPU:0, one launch (start us, length us, event | category | flops | bytes accessed | tf_op | source)
XLA Modules:
  0.0 76.4 jit_solution(13968485048439415331)
XLA Ops:
  0.0 0.8 fusion
  1.4 5.0 %shard_map.49 = bf16[512,256]{1,0:T(8,128)(2,1)} custom-call(bf16[1296,256]{1,0:T(8,128)(2,1)} %bitcast.11, bf16[36,216]{1,0:T(8,128)(2,1)} %pad_maximum_fusion.u_ref), custom_call_target="tpu_custom_call" | custom-call | flops 700000000 | bytes 8000000 | tf_op jit(solution)/shard_map/pallas_call | solution.py:255
  6.4 7.3 %all-to-all-start.2 = ((bf16[8,64,256]{2,1,0:T(8,128)(2,1)}), bf16[8,64,256]{2,1,0:T(8,128)(2,1)S(1)}, u32[]{:S(2)}, u32[]{:S(2)}) async-start(bf16[8,64,256]{2,1,0:T(8,128)(2,1)} %bitcast.15), calls=%async_computation.2 | async-start | bytes 524288 | tf_op jit(solution)/shard_map/all_to_all | solution.py:221
  14.3 2.0 %shard_map.46 = (bf16[696,256]{1,0:T(8,128)(2,1)}, bf16[696,256]{1,0:T(8,128)(2,1)}) custom-call(bf16[1296,256]{1,0:T(8,128)(2,1)} %bitcast.12, bf16[18,216]{1,0:T(8,128)(2,1)} %slice.29.u_ref), custom_call_target="tpu_custom_call" | custom-call | tf_op jit(solution)/shard_map/pallas_call | solution.py:241
  16.3 2.0 %collective-permute-start = (bf16[696,256]{1,0:T(8,128)(2,1)}, bf16[696,256]{1,0:T(8,128)(2,1)S(1)}, u32[]{:S(2)}, u32[]{:S(2)}) collective-permute-start(bf16[696,256]{1,0:T(8,128)(2,1)} %get-tuple-element.10), channel_id=1, source_target_pairs={{0,2},{2,0},{4,6},{6,4},{8,10},{10,8},{12,14},{14,12},{1,3},{3,1},... | collective-permute-start | bytes 1069064 | tf_op jit(solution)/shard_map/ppermute | solution.py:247
  18.3 3.3 %collective-permute-start.1 = (bf16[696,256]{1,0:T(8,128)(2,1)}, bf16[696,256]{1,0:T(8,128)(2,1)S(1)}, u32[]{:S(2)}, u32[]{:S(2)}) collective-permute-start(bf16[696,256]{1,0:T(8,128)(2,1)} %get-tuple-element.9.own_ref), channel_id=1, source_target_pairs={{4,0},{14,2},{8,4},{2,6},{12,8},{6,10},{0,12},{10,14},{5,1},{15,3}... | collective-permute-start | bytes 1069064 | tf_op jit(solution)/shard_map/ppermute | solution.py:248
  21.6 6.1 %collective-permute-done.across_ref = bf16[696,256]{1,0:T(8,128)(2,1)S(1)} collective-permute-done((bf16[696,256]{1,0:T(8,128)(2,1)}, bf16[696,256]{1,0:T(8,128)(2,1)S(1)}, u32[]{:S(2)}, u32[]{:S(2)}) %collective-permute-start) | collective-permute-done | bytes 356384 | tf_op jit(solution)/shard_map/ppermute | solution.py:247
  27.7 1.4 %collective-permute-done.1.along_ref = bf16[696,256]{1,0:T(8,128)(2,1)S(1)} collective-permute-done((bf16[696,256]{1,0:T(8,128)(2,1)}, bf16[696,256]{1,0:T(8,128)(2,1)S(1)}, u32[]{:S(2)}, u32[]{:S(2)}) %collective-permute-start.1) | collective-permute-done | bytes 356384 | tf_op jit(solution)/shard_map/ppermute | solution.py:248
  29.1 0.7 copy-done.5
  29.8 3.7 %shard_map.47 = bf16[256,256]{1,0:T(8,128)(2,1)} custom-call(bf16[696,256]{1,0:T(8,128)(2,1)} %get-tuple-element.9.own_ref, bf16[696,256]{1,0:T(8,128)(2,1)} %copy-done.4, bf16[696,256]{1,0:T(8,128)(2,1)} %copy-done.5), custom_call_target="tpu_custom_call" | custom-call | flops 400000000 | bytes 4000000 | tf_op jit(solution)/shard_map/pallas_call | solution.py:275
  33.5 5.0 %all-to-all-start = ((bf16[8,32,256]{2,1,0:T(8,128)(2,1)}), bf16[8,32,256]{2,1,0:T(8,128)(2,1)S(1)}, u32[]{:S(2)}, u32[]{:S(2)}) async-start(bf16[8,32,256]{2,1,0:T(8,128)(2,1)} %bitcast.16), calls=%async_computation | async-start | bytes 262144 | tf_op jit(solution)/shard_map/all_to_all | solution.py:221
  38.6 7.3 %all-to-all-done = bf16[8,32,256]{2,1,0:T(8,128)(2,1)S(1)} async-done(((bf16[8,32,256]{2,1,0:T(8,128)(2,1)}), bf16[8,32,256]{2,1,0:T(8,128)(2,1)S(1)}, u32[]{:S(2)}, u32[]{:S(2)}) %all-to-all-start) | async-done | bytes 131104 | tf_op jit(solution)/shard_map/all_to_all | solution.py:221
  45.9 0.7 broadcast_in_dim.33
  46.6 3.4 %all-to-all-start.3 = ((bf16[8,64,256]{2,1,0:T(8,128)(2,1)}), bf16[8,64,256]{2,1,0:T(8,128)(2,1)S(1)}, u32[]{:S(2)}, u32[]{:S(2)}) async-start(bf16[8,64,256]{2,1,0:T(8,128)(2,1)} %broadcast_in_dim.33), calls=%async_computation.3 | async-start | bytes 524288 | tf_op jit(solution)/shard_map/all_to_all | solution.py:225
  50.3 0.6 fusion.1
  50.9 7.3 %all-to-all-done.3 = bf16[8,64,256]{2,1,0:T(8,128)(2,1)S(1)} async-done(((bf16[8,64,256]{2,1,0:T(8,128)(2,1)}), bf16[8,64,256]{2,1,0:T(8,128)(2,1)S(1)}, u32[]{:S(2)}, u32[]{:S(2)}) %all-to-all-start.3) | async-done | bytes 262176 | tf_op jit(solution)/shard_map/all_to_all | solution.py:225
  58.2 0.7 broadcast_in_dim.32
  58.9 3.4 %all-to-all-start.1 = ((bf16[8,32,256]{2,1,0:T(8,128)(2,1)}), bf16[8,32,256]{2,1,0:T(8,128)(2,1)S(1)}, u32[]{:S(2)}, u32[]{:S(2)}) async-start(bf16[8,32,256]{2,1,0:T(8,128)(2,1)} %broadcast_in_dim.32), calls=%async_computation.1 | async-start | bytes 262144 | tf_op jit(solution)/shard_map/all_to_all | solution.py:225
  62.3 1.8 %pad_add_fusion.places_ref = s32[2]{0:T(128)} fusion(s32[1]{0:T(128)} %get-tuple-element.17, s32[1]{0:T(128)} %get-tuple-element.16), kind=kLoop, calls=%fused_computation.3 | loop fusion | flops 2 | bytes 16 | tf_op jit(solution)/shard_map/stack | solution.py:289
  64.1 0.8 %copy-done.3 = bf16[2,128,1024]{2,1,0:T(8,128)(2,1)} copy-done((bf16[2,128,1024]{2,1,0:T(8,128)(2,1)}, bf16[2,128,1024]{2,1,0:T(8,128)(2,1)S(1)}, u32[]{:S(2)}) %copy-start.3) | copy-done | bytes 524312
  64.9 2.7 %shard_map.48 = (bf16[512,512]{1,0:T(8,128)(2,1)}, bf16[512,512]{1,0:T(8,128)(2,1)}) custom-call(bf16[2,128,1024]{2,1,0:T(8,128)(2,1)} %copy-done.3), custom_call_target="tpu_custom_call" | custom-call | flops 500000000 | bytes 2000000 | tf_op jit(solution)/shard_map/pallas_call | solution.py:264
  67.7 4.6 %shard_map.50.rest_0_ = bf16[3,2,128,1024]{3,2,1,0:T(8,128)(2,1)} custom-call(s32[2]{0:T(128)} %pad_add_fusion.places_ref, bf16[512,256]{1,0:T(8,128)(2,1)} %bitcast.14, bf16[512,512]{1,0:T(8,128)(2,1)} %get-tuple-element.11.p_ref, bf16[512,512]{1,0:T(8,128)(2,1)} %get-tuple-element.12.s_ref), custom_call_target="tpu_custom_call" | custom-call | flops 1600000000 | bytes 2000000 | tf_op jit(solution)/shard_map/pallas_call | solution.py:205
  72.2 0.6 copy-done
  72.9 3.6 %shard_map.51 = bf16[3,2,128,1024]{3,2,1,0:T(8,128)(2,1)} custom-call(s32[1]{0:T(128)} %get-tuple-element.18.places_ref, bf16[256,256]{1,0:T(8,128)(2,1)} %bitcast.13, bf16[512,512]{1,0:T(8,128)(2,1)} %get-tuple-element.11.p_ref, bf16[512,512]{1,0:T(8,128)(2,1)} %get-tuple-element.12.s_ref, ...), custom_call_target="tpu_custom_call", output_to_operand_aliasing={{}: (4, {})} | custom-call | flops 800000000 | bytes 1000000 | tf_op jit(solution)/shard_map/pallas_call | solution.py:205
  (22 shorter events, 1.6 us)
Async XLA Ops:
  6.4 27.2 %all-to-all-start.2 = ((bf16[8,64,256]{2,1,0:T(8,128)(2,1)}), bf16[8,64,256]{2,1,0:T(8,128)(2,1)S(1)}, u32[]{:S(2)}, u32[]{:S(2)}) async-start(bf16[8,64,256]{2,1,0:T(8,128)(2,1)} %bitcast.15), calls=%async_computation.2 | async-start | bytes 524288 | tf_op jit(solution)/shard_map/all_to_all | solution.py:221
  16.3 33.8 %copy-start.2 = (bf16[1,2,128,1024]{3,2,1,0:T(8,128)(2,1)S(1)}, bf16[1,2,128,1024]{3,2,1,0:T(8,128)(2,1)}, u32[]{:S(2)}) copy-start(bf16[1,2,128,1024]{3,2,1,0:T(8,128)(2,1)} %param.7) | copy-start | bytes 1572868
  16.3 33.8 %copy-start.6 = (s32[3]{0:T(128)S(1)}, s32[3]{0:T(128)}, u32[]{:S(2)}) copy-start(s32[3]{0:T(128)} %param.6) | copy-start | bytes 40
  16.3 11.4 %collective-permute-start = (bf16[696,256]{1,0:T(8,128)(2,1)}, bf16[696,256]{1,0:T(8,128)(2,1)S(1)}, u32[]{:S(2)}, u32[]{:S(2)}) collective-permute-start(bf16[696,256]{1,0:T(8,128)(2,1)} %get-tuple-element.10), channel_id=1, source_target_pairs={{0,2},{2,0},{4,6},{6,4},{8,10},{10,8},{12,14},{14,12},{1,3},{3,1},... | collective-permute-start | bytes 1069064 | tf_op jit(solution)/shard_map/ppermute | solution.py:247
  18.3 10.7 %collective-permute-start.1 = (bf16[696,256]{1,0:T(8,128)(2,1)}, bf16[696,256]{1,0:T(8,128)(2,1)S(1)}, u32[]{:S(2)}, u32[]{:S(2)}) collective-permute-start(bf16[696,256]{1,0:T(8,128)(2,1)} %get-tuple-element.9.own_ref), channel_id=1, source_target_pairs={{4,0},{14,2},{8,4},{2,6},{12,8},{6,10},{0,12},{10,14},{5,1},{15,3}... | collective-permute-start | bytes 1069064 | tf_op jit(solution)/shard_map/ppermute | solution.py:248
  27.7 1.4 %copy-start.4 = (bf16[696,256]{1,0:T(8,128)(2,1)}, bf16[696,256]{1,0:T(8,128)(2,1)S(1)}, u32[]{:S(2)}) copy-start(bf16[696,256]{1,0:T(8,128)(2,1)S(1)} %collective-permute-done.across_ref) | copy-start | bytes 1069060
  29.1 0.7 copy-start.5
  33.5 12.4 %all-to-all-start = ((bf16[8,32,256]{2,1,0:T(8,128)(2,1)}), bf16[8,32,256]{2,1,0:T(8,128)(2,1)S(1)}, u32[]{:S(2)}, u32[]{:S(2)}) async-start(bf16[8,32,256]{2,1,0:T(8,128)(2,1)} %bitcast.16), calls=%async_computation | async-start | bytes 262144 | tf_op jit(solution)/shard_map/all_to_all | solution.py:221
  46.6 11.6 %all-to-all-start.3 = ((bf16[8,64,256]{2,1,0:T(8,128)(2,1)}), bf16[8,64,256]{2,1,0:T(8,128)(2,1)S(1)}, u32[]{:S(2)}, u32[]{:S(2)}) async-start(bf16[8,64,256]{2,1,0:T(8,128)(2,1)} %broadcast_in_dim.33), calls=%async_computation.3 | async-start | bytes 524288 | tf_op jit(solution)/shard_map/all_to_all | solution.py:225
  50.1 14.1 %collective-permute-start.2 = (bf16[2,128,1024]{2,1,0:T(8,128)(2,1)S(1)}, bf16[2,128,1024]{2,1,0:T(8,128)(2,1)S(1)}, u32[]{:S(2)}, u32[]{:S(2)}) collective-permute-start(bf16[2,128,1024]{2,1,0:T(8,128)(2,1)S(1)} %bitcast.17), channel_id=1, source_target_pairs={{1,0},{0,1},{3,2},{2,3},{5,4},{4,5},{7,6},{6,7},{9,8},{8,9},{11,10... | collective-permute-start | bytes 1572872 | tf_op jit(solution)/shard_map/ppermute | solution.py:253
  58.2 9.4 %copy-start.1 = (bf16[8,64,256]{2,1,0:T(8,128)(2,1)}, bf16[8,64,256]{2,1,0:T(8,128)(2,1)S(1)}, u32[]{:S(2)}) copy-start(bf16[8,64,256]{2,1,0:T(8,128)(2,1)S(1)} %all-to-all-done.3) | copy-start | bytes 786436
  58.9 13.3 %all-to-all-start.1 = ((bf16[8,32,256]{2,1,0:T(8,128)(2,1)}), bf16[8,32,256]{2,1,0:T(8,128)(2,1)S(1)}, u32[]{:S(2)}, u32[]{:S(2)}) async-start(bf16[8,32,256]{2,1,0:T(8,128)(2,1)} %broadcast_in_dim.32), calls=%async_computation.1 | async-start | bytes 262144 | tf_op jit(solution)/shard_map/all_to_all | solution.py:225
  64.1 0.8 %copy-start.3 = (bf16[2,128,1024]{2,1,0:T(8,128)(2,1)}, bf16[2,128,1024]{2,1,0:T(8,128)(2,1)S(1)}, u32[]{:S(2)}) copy-start(bf16[2,128,1024]{2,1,0:T(8,128)(2,1)S(1)} %collective-permute-done.2.p_ref) | copy-start | bytes 1572868
  72.2 0.6 copy-start

commit v2 on v1

--- a/solution.py
+++ b/solution.py
@@ -7,12 +7,15 @@
 from jax.experimental.pallas import tpu as pltpu
 from jax.sharding import PartitionSpec as P
 
+
 SPIN = 4
 LX = 9
 LZ = 24
 F32 = jnp.float32
 BF16 = jnp.bfloat16
 VMEM = pl.BlockSpec(memory_space=pltpu.VMEM)
+ANY = pl.BlockSpec(memory_space=pl.ANY)
+PARAMS = pltpu.CompilerParams(vmem_limit_bytes=12 * 1024 * 1024)
 
 
 def half_rows(sites):
@@ -63,13 +66,13 @@
     overlap = 2 * half - sites
     vectors = v_ref.shape[1]
     parity = lax.rem(lax.axis_index("space"), 2)
-    entries = u_ref.shape[0]
+    entries = 18
 
     def fill(ref, upper):
         first = sites - half if upper else 0
         for comp in range(6):
             ref[pl.ds(comp * half, half), :] = v_ref[pl.ds(comp * sites + first, half), :]
-        links = u_ref[:, first : first + half].astype(F32)
+        links = u_ref[18:36, first : first + half].astype(F32)
         if upper and overlap:
             lane = lax.broadcasted_iota(jnp.int32, links.shape, 1)
             links = jnp.where(lane < overlap, 0.0, links)
@@ -106,7 +109,7 @@
         ahead = (slab * LX + (along + 1) % LX) * LZ
         for comp, value in enumerate(adjoint_product(here, 0, vec)):
             w_ref[0, pl.ds(comp * sites + ahead, LZ), :] = value
-        for comp, value in enumerate(adjoint_product(here, 18, vec)):
+        for comp, value in enumerate(adjoint_product(here, 36, vec)):
             w_ref[1, pl.ds(comp * sites + start, LZ), :] = pltpu.roll(value, 1, 0)
     real = pl.ds(0, 3 * sites)
     imag = pl.ds(3 * sites, 3 * sites)
@@ -120,7 +123,7 @@
         o_ref[pl.ds(index * vectors, vectors), :] = packed.astype(BF16)
 
 
-def middle_kernel(half, own_ref, across_ref, along_ref, o_ref, w_ref):
+def middle_kernel(half, own_ref, across_ref, along_ref, flat_ref, o_ref, w_ref, pack_ref, sem):
     even = lax.rem(lax.axis_index("space"), 2) == 0
     first = jnp.where(even, own_ref[...], along_ref[...])
     last = jnp.where(even, along_ref[...], own_ref[...])
@@ -135,7 +138,12 @@
     v_real = jnp.concatenate([middle[: 3 * half], last[: 3 * half]], axis=0)
     v_imag = jnp.concatenate([middle[3 * half : 6 * half], last[3 * half : 6 * half]], axis=0)
     packed = packed_elemental(w_ref[0].astype(BF16), w_ref[1].astype(BF16), v_real, v_imag)
-    o_ref[...] = packed.astype(BF16)
+    del flat_ref
+    pack_ref[...] = packed.astype(BF16)
+    vectors = packed.shape[0]
+    copy = pltpu.make_async_copy(pack_ref, o_ref.at[pl.ds(2 * vectors, vectors)], sem)
+    copy.start()
+    copy.wait()
 
 
 def spread(size):
@@ -188,47 +196,43 @@
             ).astype(BF16)
 
 
-def last_call(places, packed, spins, table, shape, result=None):
+def last_call(dirs, packed, spins, table, shape):
     vectors = packed.shape[1]
-    count = packed.shape[0] // vectors
-    specs = [
-        pl.BlockSpec((vectors, vectors), lambda i, at: (i, 0)),
-        pl.BlockSpec(spins.shape, lambda i, at: (0, 0)),
-        pl.BlockSpec(table.shape, lambda i, at: (0, 0)),
-    ]
-    args = [places, packed, spins, table]
-    aliases = {}
-    if result is not None:
-        specs.append(pl.BlockSpec(memory_space=pl.ANY))
-        args.append(result)
-        aliases = {4: 0}
+
+    def place(direction, dirs_ref):
+        at = jnp.where(dirs_ref[1] == direction, 1, jnp.where(dirs_ref[2] == direction, 2, 0))
+        return at, 0, 0, 0
+
     return pl.pallas_call(
         last_kernel,
         grid_spec=pltpu.PrefetchScalarGridSpec(
             num_scalar_prefetch=1,
-            grid=(count,),
-            in_specs=specs,
-            out_specs=pl.BlockSpec((1,) + shape[1:], lambda i, at: (at[i], 0, 0, 0)),
+            grid=(shape[0],),
+            in_specs=[
+                pl.BlockSpec((vectors, vectors), lambda i, at: (lax.rem(2 * i, 3), 0)),
+                VMEM,
+                VMEM,
+            ],
+            out_specs=pl.BlockSpec((1,) + shape[1:], place),
         ),
         out_shape=jax.ShapeDtypeStruct(shape, BF16),
-        input_output_aliases=aliases,
-        cost_estimate=pl.CostEstimate(flops=count * 800_000_000, bytes_accessed=count * 1_000_000, transcendentals=0),
-    )(*args)
+        cost_estimate=pl.CostEstimate(
+            flops=2_400_000_000, bytes_accessed=3_000_000, transcendentals=0
+        ),
+        compiler_params=PARAMS,
+    )(dirs, packed, spins, table)
 
 
 def sum_over_space(partial, ranks):
     rows, width = partial.shape
-    pieces = lax.all_to_all(
-        partial.reshape(ranks, rows // ranks, width), "space", 0, 0, tiled=True
-    )
+    pieces = lax.all_to_all(partial.reshape(ranks, rows // ranks, width), "space", 0, 0, tiled=True)
     total = jnp.sum(pieces.astype(F32), axis=0).astype(BF16)
-    whole = lax.all_to_all(
-        jnp.broadcast_to(total[None], (ranks,) + total.shape), "space", 0, 0, tiled=True
-    )
+    spread_out = jnp.broadcast_to(total[None], (ranks,) + total.shape)
+    whole = lax.all_to_all(spread_out, "space", 0, 0, tiled=True)
     return whole.reshape(rows, width)
 
 
-def on_device(eigvecs, links, dirs, peram):
+def blocks(eigvecs, links, dirs, peram):
     ranks = lax.axis_size("space")
     vectors, sites = eigvecs.shape[2], eigvecs.shape[4]
     assert sites == LX * LZ and ranks % 2 == 0
@@ -243,7 +247,8 @@
         out_shape=(payload, payload),
         in_specs=[VMEM] * 2,
         out_specs=(VMEM, VMEM),
-    )(field, link_rows[18:36])
+        compiler_params=PARAMS,
+    )(field, link_rows)
     from_across = lax.ppermute(across, "space", [(i, i ^ 1) for i in range(ranks)])
     from_along = lax.ppermute(
         along,
@@ -252,14 +257,15 @@
     )
     partner = lax.ppermute(peram[0], "tm", [((i + 1) % 2, i) for i in range(2)])
 
-    flat = pl.pallas_call(
+    packed = pl.pallas_call(
         functools.partial(front_kernel, sites),
-        out_shape=jax.ShapeDtypeStruct((2 * vectors, vectors), BF16),
+        out_shape=jax.ShapeDtypeStruct((3 * vectors, vectors), BF16),
         in_specs=[VMEM] * 2,
         out_specs=VMEM,
         scratch_shapes=[pltpu.VMEM((2, 6 * sites, vectors), F32)],
         cost_estimate=pl.CostEstimate(flops=700_000_000, bytes_accessed=8_000_000, transcendentals=0),
-    )(field, jnp.concatenate([link_rows[:18], link_rows[36:]]))
+        compiler_params=PARAMS,
+    )(field, link_rows)
     columns = partner.shape[1]
     spins, table = pl.pallas_call(
         spins_kernel,
@@ -270,24 +276,27 @@
         in_specs=[VMEM],
         out_specs=(VMEM, VMEM),
         cost_estimate=pl.CostEstimate(flops=500_000_000, bytes_accessed=2_000_000, transcendentals=0),
+        compiler_params=PARAMS,
     )(partner)
-    whole_flat = sum_over_space(flat, ranks)
-    upright = pl.pallas_call(
+    packed = pl.pallas_call(
         functools.partial(middle_kernel, half),
-        out_shape=jax.ShapeDtypeStruct((vectors, vectors), BF16),
-        in_specs=[VMEM] * 3,
-        out_specs=VMEM,
-        scratch_shapes=[pltpu.VMEM((2, 6 * half, vectors), F32)],
-        cost_estimate=pl.CostEstimate(flops=400_000_000, bytes_accessed=4_000_000, transcendentals=0),
-    )(along, from_across, from_along)
-    whole_upright = sum_over_space(upright, ranks)
-
-    count = dirs.shape[0]
-    order = jnp.arange(count, dtype=jnp.int32)
-    places = jnp.sum(jnp.where(dirs[None, :] == order[:, None], order[None, :], 0), axis=1)
-    shape = (count, 2, columns, SPIN * vectors)
-    result = last_call(jnp.stack([places[0], places[2]]), whole_flat, spins, table, shape)
-    result = last_call(places[1:2], whole_upright, spins, table, shape, result)
+        out_shape=jax.ShapeDtypeStruct((3 * vectors, vectors), BF16),
+        in_specs=[VMEM] * 3 + [ANY],
+        out_specs=ANY,
+        scratch_shapes=[
+            pltpu.VMEM((2, 6 * half, vectors), F32),
+            pltpu.VMEM((vectors, vectors), BF16),
+            pltpu.SemaphoreType.DMA,
+        ],
+        input_output_aliases={3: 0},
+        cost_estimate=pl.CostEstimate(
+            flops=400_000_000, bytes_accessed=4_000_000, transcendentals=0
+        ),
+        compiler_params=PARAMS,
+    )(along, from_across, from_along, packed)
+    packed = sum_over_space(packed, ranks)
+    shape = (dirs.shape[0], 2, columns, SPIN * vectors)
+    result = last_call(dirs, packed, spins, table, shape)
     return result[None]
 
 
@@ -299,7 +308,7 @@
         P(("parts", "tm"), None, "space", None),
     )
     return jax.shard_map(
-        on_device,
+        blocks,
         mesh=mesh,
         in_specs=placed,
         out_specs=P(("parts", "tm"), None, None, "space", None),

time: 77.2 us -> 54.2 us (0.70)
  blocking collectives: 0 us -> 16.4 us
  starting transfers between devices: 24.4 us -> 10.1 us
  Pallas kernels: 21.6 us -> 10.4 us
  waiting for transfers between devices: 22.1 us -> 14.1 us
  local copies, waits for them, and re-layouts: 5.63 us -> 2.66 us
  other arithmetic: 2.63 us -> 0.06 us
    all_to_all x0 -> x1, blocking collectives: none -> 16.4 us  [sum_over_space(): lax.all_to_all(partial.reshape(ranks, rows // ranks, width), 'space', 0,...]
    all_to_all x4 -> x1, starting transfers between devices: 19.1 us -> 3.45 us  [sum_over_space(): whole = lax.all_to_all(spread_out, 'space', 0, 0, tiled=True)]
    pallas_call x4, Pallas kernels: 13.4 us -> 6.2 us  [the longest x1 3.17 us: blocks(): pl.pallas_call(functools.partial(front_kernel, sites), out_shape=jax.Shap...]
    all_to_all x4 -> x1, waiting for transfers between devices: 14.6 us -> 8.09 us  [sum_over_space(): whole = lax.all_to_all(spread_out, 'space', 0, 0, tiled=True)]
    pallas_call x2 -> x1, Pallas kernels: 8.14 us -> 4.16 us  [last_call(): pl.pallas_call(last_kernel, grid_spec=pltpu.PrefetchScalarGridSpec(num_sc...]
    slice x5 -> x0, local copies, waits for them, and re-layouts: 2.04 us -> none  [the longest x2 0.78 us: on_device(): link_rows[:18]]
    another operation x1 -> x0, other arithmetic: 1.84 us -> none  [on_device(): jnp.stack([places[0], places[2]])]
    ppermute x3, waiting for transfers between devices: 7.48 us -> 6.02 us  [the longest x1 2.58 us: blocks(): lax.ppermute(along, 'space', [((i + 2) % ranks if i % 2 == 0 else (i - 2)...]
  transfers between devices with their start and end apart: 7 -> 4, of which waited for: 4 -> 4; matrix products, arithmetic and copies ran while one was open for 5% -> 0% of each run, Pallas kernels for 17% -> 8%
where the time goes in v2:
time: 54.2 us; the launch traced here: 53.8 us
  blocking collectives  16.4 us (30%)
  waiting for transfers between devices  14.1 us (26%)
  Pallas kernels  10.4 us (19%)
  starting transfers between devices  10.1 us (19%)
  local copies, waits for them, and re-layouts  2.66 us (5%)
    all_to_all x1, blocking collectives, sum_over_space(): lax.all_to_all(partial.reshape(ranks, rows // ranks, width), 'space', 0,...  16.4 us
    all_to_all x1, waiting for transfers between devices, sum_over_space(): whole = lax.all_to_all(spread_out, 'space', 0, 0, tiled=True)  8.09 us
    pallas_call x1, Pallas kernels, last_call(): pl.pallas_call(last_kernel, grid_spec=pltpu.PrefetchScalarGridSpec(num_sc...  4.16 us
    ppermute x1, starting transfers between devices, blocks(): lax.ppermute(along, 'space', [((i + 2) % ranks if i % 2 == 0 else (i - 2)...  3.6 us
    all_to_all x1, starting transfers between devices, sum_over_space(): whole = lax.all_to_all(spread_out, 'space', 0, 0, tiled=True)  3.45 us
    pallas_call x1, Pallas kernels, blocks(): pl.pallas_call(functools.partial(front_kernel, sites), out_shape=jax.Shap...  3.17 us
    ppermute x1, starting transfers between devices, blocks(): lax.ppermute(across, 'space', [(i, i ^ 1) for i in range(ranks)])  3.01 us
    ppermute x1, waiting for transfers between devices, blocks(): lax.ppermute(along, 'space', [((i + 2) % ranks if i % 2 == 0 else (i - 2)...  2.58 us
  transfers between devices with their start and end apart: 4, of which 4 were waited for; matrix products, arithmetic and copies ran while one was open for 0% of the time, Pallas kernels for 8%

profile of v2, /device:TPU:0, one launch (start us, length us, event | category | flops | bytes accessed | tf_op | source)
XLA Modules:
  0.0 53.8 jit_solution(14703291416458120268)
XLA Ops:
  0.0 0.8 %reshape_squeeze.3.u_ref = bf16[54,216]{1,0:T(8,128)(2,1)S(1)} reshape(bf16[1,3,3,3,2,216]{5,4,3,2,1,0:T(2,128)(2,1)} %param.5) | data formatting | bytes 46656 | tf_op jit(solution)/shard_map/reshape;squeeze | solution.py:240
  0.8 0.0 copy-start
  0.8 1.1 %copy-done = bf16[1,2,256,3,216]{2,4,3,1,0:T(8,128)(2,1)S(1)} copy-done((bf16[1,2,256,3,216]{2,4,3,1,0:T(8,128)(2,1)S(1)}, bf16[1,2,256,3,216]{2,4,3,1,0:T(8,128)(2,1)}, u32[]{:S(2)}) %copy-start) | copy-done | bytes 663576
  1.9 0.1 shard_map.46
  2.0 3.0 %collective-permute-start = (bf16[696,256]{1,0:T(8,128)(2,1)S(1)}, bf16[696,256]{1,0:T(8,128)(2,1)S(1)}, u32[]{:S(2)}, u32[]{:S(2)}) collective-permute-start(bf16[696,256]{1,0:T(8,128)(2,1)S(1)} %get-tuple-element.10), channel_id=1, source_target_pairs={{0,2},{2,0},{4,6},{6,4},{8,10},{10,8},{12,14},{14,12},{1,3},{3,1},... | collective-permute-start | bytes 1069064 | tf_op jit(solution)/shard_map/ppermute | solution.py:252
  5.0 3.6 %collective-permute-start.1 = (bf16[696,256]{1,0:T(8,128)(2,1)S(1)}, bf16[696,256]{1,0:T(8,128)(2,1)S(1)}, u32[]{:S(2)}, u32[]{:S(2)}) collective-permute-start(bf16[696,256]{1,0:T(8,128)(2,1)S(1)} %get-tuple-element.9.own_ref), channel_id=1, source_target_pairs={{4,0},{14,2},{8,4},{2,6},{12,8},{6,10},{0,12},{10,14},{5,1},{15,3}... | collective-permute-start | bytes 1069064 | tf_op jit(solution)/shard_map/ppermute | solution.py:253
  8.6 3.2 %shard_map.47.flat_ref = bf16[768,256]{1,0:T(8,128)(2,1)S(1)} custom-call(bf16[1296,256]{1,0:T(8,128)(2,1)S(1)} %bitcast.11, bf16[54,216]{1,0:T(8,128)(2,1)S(1)} %reshape_squeeze.3.u_ref), custom_call_target="tpu_custom_call" | custom-call | flops 700000000 | bytes 8000000 | tf_op jit(solution)/shard_map/pallas_call | solution.py:260
  11.8 1.5 %collective-permute-done.across_ref = bf16[696,256]{1,0:T(8,128)(2,1)S(1)} collective-permute-done((bf16[696,256]{1,0:T(8,128)(2,1)S(1)}, bf16[696,256]{1,0:T(8,128)(2,1)S(1)}, u32[]{:S(2)}, u32[]{:S(2)}) %collective-permute-start) | collective-permute-done | bytes 356384 | tf_op jit(solution)/shard_map/ppermute | solution.py:252
  13.3 2.6 %collective-permute-done.1.along_ref = bf16[696,256]{1,0:T(8,128)(2,1)S(1)} collective-permute-done((bf16[696,256]{1,0:T(8,128)(2,1)S(1)}, bf16[696,256]{1,0:T(8,128)(2,1)S(1)}, u32[]{:S(2)}, u32[]{:S(2)}) %collective-permute-start.1) | collective-permute-done | bytes 356384 | tf_op jit(solution)/shard_map/ppermute | solution.py:253
  15.9 2.1 %shard_map.48 = bf16[768,256]{1,0:T(8,128)(2,1)S(1)} custom-call(bf16[696,256]{1,0:T(8,128)(2,1)S(1)} %get-tuple-element.9.own_ref, bf16[696,256]{1,0:T(8,128)(2,1)S(1)} %collective-permute-done.across_ref, bf16[696,256]{1,0:T(8,128)(2,1)S(1)} %collective-permute-done.1.along_ref, ...), custom_call_target="tpu_custom_call", output_to_operand_aliasing={{}: (3, {})} | custom-call | flops 400000000 | bytes 4000000 | tf_op jit(solution)/shard_map/pallas_call | solution.py:281
  18.0 0.0 copy-start.2
  18.0 16.4 %all_to_all.10 = bf16[8,96,256]{2,1,0:T(8,128)(2,1)S(1)} all-to-all(bf16[8,96,256]{2,1,0:T(8,128)(2,1)S(1)} %bitcast.9), channel_id=1, replica_groups=mesh['parts'=2,'space'=8,'tm'=2] {'space'}, dimensions={0} | all-to-all | bytes 786432 | tf_op jit(solution)/shard_map/all_to_all | solution.py:228
  34.4 0.1 reduce_sum.12
  34.4 0.0 copy-start.1
  34.5 0.8 %broadcast_in_dim.4 = bf16[8,96,256]{2,1,0:T(8,128)(2,1)} broadcast(bf16[96,256]{1,0:T(8,128)(2,1)S(1)} %reduce_sum.12), dimensions={1,2} | broadcast | bytes 442368 | tf_op jit(solution)/shard_map/broadcast_in_dim | solution.py:230
  35.2 3.5 %all-to-all-start.1 = ((bf16[8,96,256]{2,1,0:T(8,128)(2,1)}), bf16[8,96,256]{2,1,0:T(8,128)(2,1)S(1)}, u32[]{:S(2)}, u32[]{:S(2)}) async-start(bf16[8,96,256]{2,1,0:T(8,128)(2,1)} %broadcast_in_dim.4), calls=%async_computation.1 | async-start | bytes 786432 | tf_op jit(solution)/shard_map/all_to_all | solution.py:231
  38.7 0.0 copy-done.2
  38.7 0.1 collective-permute-start.2
  38.8 1.9 %collective-permute-done.2.p_ref = bf16[2,128,1024]{2,1,0:T(8,128)(2,1)S(1)} collective-permute-done((bf16[2,128,1024]{2,1,0:T(8,128)(2,1)S(1)}, bf16[2,128,1024]{2,1,0:T(8,128)(2,1)S(1)}, u32[]{:S(2)}, u32[]{:S(2)}) %collective-permute-start.2) | collective-permute-done | bytes 524320 | tf_op jit(solution)/shard_map/ppermute | solution.py:258
  40.7 0.9 %shard_map.49 = (bf16[512,512]{1,0:T(8,128)(2,1)S(1)}, bf16[512,512]{1,0:T(8,128)(2,1)S(1)}) custom-call(bf16[2,128,1024]{2,1,0:T(8,128)(2,1)S(1)} %collective-permute-done.2.p_ref), custom_call_target="tpu_custom_call" | custom-call | flops 500000000 | bytes 2000000 | tf_op jit(solution)/shard_map/pallas_call | solution.py:270
  41.6 8.1 %all-to-all-done.1 = bf16[8,96,256]{2,1,0:T(8,128)(2,1)S(1)} async-done(((bf16[8,96,256]{2,1,0:T(8,128)(2,1)}), bf16[8,96,256]{2,1,0:T(8,128)(2,1)S(1)}, u32[]{:S(2)}, u32[]{:S(2)}) %all-to-all-start.1) | async-done | bytes 393248 | tf_op jit(solution)/shard_map/all_to_all | solution.py:231
  49.7 0.0 copy-done.1
  49.7 4.2 %shard_map.50 = bf16[3,2,128,1024]{3,2,1,0:T(8,128)(2,1)} custom-call(s32[3]{0:T(128)S(1)} %copy-done.1, bf16[768,256]{1,0:T(8,128)(2,1)S(1)} %bitcast.12, bf16[512,512]{1,0:T(8,128)(2,1)S(1)} %get-tuple-element.11.p_ref, bf16[512,512]{1,0:T(8,128)(2,1)S(1)} %get-tuple-element.12.s_ref), custom_call_target="tpu_custom_call" | custom-call | flops 2400000000 | bytes 3000000 | tf_op jit(solution)/shard_map/pallas_call | solution.py:206
Async XLA Ops:
  0.8 1.1 %copy-start = (bf16[1,2,256,3,216]{2,4,3,1,0:T(8,128)(2,1)S(1)}, bf16[1,2,256,3,216]{2,4,3,1,0:T(8,128)(2,1)}, u32[]{:S(2)}) copy-start(bf16[1,2,256,3,216]{2,4,3,1,0:T(8,128)(2,1)} %param.4) | copy-start | bytes 1990660
  2.0 11.3 %collective-permute-start = (bf16[696,256]{1,0:T(8,128)(2,1)S(1)}, bf16[696,256]{1,0:T(8,128)(2,1)S(1)}, u32[]{:S(2)}, u32[]{:S(2)}) collective-permute-start(bf16[696,256]{1,0:T(8,128)(2,1)S(1)} %get-tuple-element.10), channel_id=1, source_target_pairs={{0,2},{2,0},{4,6},{6,4},{8,10},{10,8},{12,14},{14,12},{1,3},{3,1},... | collective-permute-start | bytes 1069064 | tf_op jit(solution)/shard_map/ppermute | solution.py:252
  5.0 10.9 %collective-permute-start.1 = (bf16[696,256]{1,0:T(8,128)(2,1)S(1)}, bf16[696,256]{1,0:T(8,128)(2,1)S(1)}, u32[]{:S(2)}, u32[]{:S(2)}) collective-permute-start(bf16[696,256]{1,0:T(8,128)(2,1)S(1)} %get-tuple-element.9.own_ref), channel_id=1, source_target_pairs={{4,0},{14,2},{8,4},{2,6},{12,8},{6,10},{0,12},{10,14},{5,1},{15,3}... | collective-permute-start | bytes 1069064 | tf_op jit(solution)/shard_map/ppermute | solution.py:253
  18.0 20.7 %copy-start.2 = (bf16[1,2,128,1024]{3,2,1,0:T(8,128)(2,1)S(1)}, bf16[1,2,128,1024]{3,2,1,0:T(8,128)(2,1)}, u32[]{:S(2)}) copy-start(bf16[1,2,128,1024]{3,2,1,0:T(8,128)(2,1)} %param.7) | copy-start | bytes 1572868
  34.4 15.2 %copy-start.1 = (s32[3]{0:T(128)S(1)}, s32[3]{0:T(128)}, u32[]{:S(2)}) copy-start(s32[3]{0:T(128)} %places_ref.1) | copy-start | bytes 40
  35.2 14.4 %all-to-all-start.1 = ((bf16[8,96,256]{2,1,0:T(8,128)(2,1)}), bf16[8,96,256]{2,1,0:T(8,128)(2,1)S(1)}, u32[]{:S(2)}, u32[]{:S(2)}) async-start(bf16[8,96,256]{2,1,0:T(8,128)(2,1)} %broadcast_in_dim.4), calls=%async_computation.1 | async-start | bytes 786432 | tf_op jit(solution)/shard_map/all_to_all | solution.py:231
  38.7 2.0 %collective-permute-start.2 = (bf16[2,128,1024]{2,1,0:T(8,128)(2,1)S(1)}, bf16[2,128,1024]{2,1,0:T(8,128)(2,1)S(1)}, u32[]{:S(2)}, u32[]{:S(2)}) collective-permute-start(bf16[2,128,1024]{2,1,0:T(8,128)(2,1)S(1)} %bitcast.13), channel_id=1, source_target_pairs={{1,0},{0,1},{3,2},{2,3},{5,4},{4,5},{7,6},{6,7},{9,8},{8,9},{11,10... | collective-permute-start | bytes 1572872 | tf_op jit(solution)/shard_map/ppermute | solution.py:258

commit v3 on v2

--- a/solution.py
+++ b/solution.py
@@ -15,6 +15,8 @@
 BF16 = jnp.bfloat16
 VMEM = pl.BlockSpec(memory_space=pltpu.VMEM)
 ANY = pl.BlockSpec(memory_space=pl.ANY)
+HBM = pl.BlockSpec(memory_space=pltpu.HBM)
+VMEM_BYTES = 67_043_328
 PARAMS = pltpu.CompilerParams(vmem_limit_bytes=12 * 1024 * 1024)
 
 
@@ -61,46 +63,48 @@
     return (real + imag) + jnp.transpose(imag - real)
 
 
-def prepare_kernel(sites, v_ref, u_ref, across_ref, along_ref):
+def link_table(u_ref, first, last):
+    return jnp.concatenate([u_ref[at].astype(F32) for at in range(first, last)], axis=0)
+
+
+def prepare_kernel(sites, v_ref, u_ref, across_ref, along_ref, link_ref, sems, link_sem):
     half = half_rows(sites)
     overlap = 2 * half - sites
     vectors = v_ref.shape[1]
     parity = lax.rem(lax.axis_index("space"), 2)
-    entries = 18
-
-    def fill(ref, upper):
-        first = sites - half if upper else 0
+    fetch = pltpu.make_async_copy(u_ref.at[pl.ds(9, 9)], link_ref, link_sem)
+    fetch.start()
+    copies = []
+    for slot, (ref, upper) in enumerate(((across_ref, 1 - parity), (along_ref, parity))):
         for comp in range(6):
-            ref[pl.ds(comp * half, half), :] = v_ref[pl.ds(comp * sites + first, half), :]
-        links = u_ref[18:36, first : first + half].astype(F32)
-        if upper and overlap:
-            lane = lax.broadcasted_iota(jnp.int32, links.shape, 1)
-            links = jnp.where(lane < overlap, 0.0, links)
-        rows = ref.shape[0] - 6 * half
-        block = jnp.concatenate(
-            [
-                jnp.concatenate([links, jnp.zeros((rows - entries, half), F32)], axis=0),
-                jnp.zeros((rows, vectors - half), F32),
-            ],
-            axis=1,
-        )
+            first = pl.multiple_of(comp * sites + upper * (sites - half), 8)
+            copy = pltpu.make_async_copy(
+                v_ref.at[pl.ds(first, half)],
+                ref.at[pl.ds(comp * half, half)],
+                sems.at[slot, comp],
+            )
+            copy.start()
+            copies.append(copy)
+    fetch.wait()
+    links = link_table(link_ref, 0, 9)
+    rows = across_ref.shape[0] - 6 * half
+    lower = links[:, :half]
+    upper = links[:, sites - half :]
+    lane = lax.broadcasted_iota(jnp.int32, upper.shape, 1)
+    upper = jnp.where(lane < overlap, 0.0, upper)
+    for ref, wanted in ((across_ref, 1 - parity), (along_ref, parity)):
+        block = jnp.where(wanted == 1, upper, lower)
+        block = jnp.concatenate([block, jnp.zeros((rows - block.shape[0], half), F32)], axis=0)
+        block = jnp.concatenate([block, jnp.zeros((rows, vectors - half), F32)], axis=1)
         ref[pl.ds(6 * half, rows), :] = block.astype(BF16)
-
-    @pl.when(parity == 0)
-    def _():
-        fill(across_ref, True)
-        fill(along_ref, False)
-
-    @pl.when(parity == 1)
-    def _():
-        fill(across_ref, False)
-        fill(along_ref, True)
+    for copy in copies:
+        copy.wait()
 
 
 def front_kernel(sites, v_ref, u_ref, o_ref, w_ref):
     planes = sites // LZ
     vectors = v_ref.shape[1]
-    columns = dot(identity(sites), u_ref[...], 1, 1)
+    columns = dot(identity(sites), link_table(u_ref, 0, 27).astype(BF16), 1, 1)
     for plane in range(planes):
         slab, along = plane // LX, plane % LX
         start = plane * LZ
@@ -153,50 +157,51 @@
     return jnp.where(cols == target, 1.0, 0.0).astype(BF16)
 
 
-def spins_kernel(p_ref, o_ref, s_ref):
+def spins_kernel(p_ref, minus_ref, plus_ref, s_ref):
     columns, wide = p_ref.shape[1], p_ref.shape[2]
     vectors = wide // SPIN
-    block = 128
+    block = s_ref.shape[0] // SPIN
     table = spread(block)
     s_ref[...] = table
-    for part in range(2):
-        for chunk in range(vectors // block):
-            piece = p_ref[part, :, pl.ds(chunk * block * SPIN, block * SPIN)]
-            apart = dot(piece, table, 1, 1).astype(BF16)
-            for spin in range(SPIN):
-                o_ref[
-                    pl.ds(spin * columns, columns),
-                    pl.ds(part * vectors + chunk * block, block),
-                ] = apart[:, spin * block : (spin + 1) * block]
-
-
-def last_kernel(places_ref, m_ref, p_ref, s_ref, *rest):
-    o_ref = rest[-1]
+    for chunk in range(vectors // block):
+        at = pl.ds(chunk * block * SPIN, block * SPIN)
+        real = dot(p_ref[0, :, at], table, 1, 1)
+        imag = dot(p_ref[1, :, at], table, 1, 1)
+        less = (0.5 * (real - imag)).astype(BF16)
+        more = (0.5 * (real + imag)).astype(BF16)
+        to = pl.ds(chunk * block, block)
+        for spin in range(SPIN):
+            lanes = slice(spin * block, (spin + 1) * block)
+            rows = pl.ds(2 * spin * columns, columns)
+            below = pl.ds((2 * spin + 1) * columns, columns)
+            minus_ref[rows, to] = less[:, lanes]
+            minus_ref[below, to] = more[:, lanes]
+            plus_ref[rows, to] = -more[:, lanes]
+            plus_ref[below, to] = less[:, lanes]
+
+
+def last_kernel(places_ref, m_ref, minus_ref, plus_ref, s_ref, o_ref):
     columns = o_ref.shape[2]
     vectors = m_ref.shape[1]
     block = s_ref.shape[0] // SPIN
-    packed = m_ref[...].astype(F32)
-    turned = jnp.transpose(packed)
-    real = (0.5 * (turned - packed)).astype(BF16)
-    imag = (0.5 * (packed + turned)).astype(BF16)
-    minus = -imag
-    right = jnp.concatenate(
-        [jnp.concatenate([real, imag], axis=1), jnp.concatenate([minus, real], axis=1)], axis=0
-    )
-    product = dot(p_ref[...], right, 1, 0).astype(BF16)
-    for part in range(2):
-        for chunk in range(vectors // block):
-            at = part * vectors + chunk * block
-            piece = jnp.concatenate(
-                [product[spin * columns : (spin + 1) * columns, at : at + block] for spin in range(SPIN)],
-                axis=1,
-            )
-            o_ref[0, part, :, pl.ds(chunk * block * SPIN, block * SPIN)] = dot(
-                piece, s_ref[...], 1, 0
-            ).astype(BF16)
-
-
-def last_call(dirs, packed, spins, table, shape):
+    packed = m_ref[...]
+    product = (dot(minus_ref[...], packed, 1, 1) + dot(plus_ref[...], packed, 1, 0)).astype(BF16)
+    for chunk in range(vectors // block):
+        at = chunk * block
+        piece = jnp.concatenate(
+            [
+                product[2 * spin * columns : 2 * (spin + 1) * columns, at : at + block]
+                for spin in range(SPIN)
+            ],
+            axis=1,
+        )
+        apart = dot(piece, s_ref[...], 1, 0).astype(BF16)
+        to = pl.ds(at * SPIN, block * SPIN)
+        o_ref[0, 0, :, to] = apart[:columns]
+        o_ref[0, 1, :, to] = apart[columns:]
+
+
+def last_call(dirs, packed, minus, plus, table, shape):
     vectors = packed.shape[1]
 
     def place(direction, dirs_ref):
@@ -210,6 +215,7 @@
             grid=(shape[0],),
             in_specs=[
                 pl.BlockSpec((vectors, vectors), lambda i, at: (lax.rem(2 * i, 3), 0)),
+                VMEM,
                 VMEM,
                 VMEM,
             ],
@@ -220,15 +226,29 @@
             flops=2_400_000_000, bytes_accessed=3_000_000, transcendentals=0
         ),
         compiler_params=PARAMS,
-    )(dirs, packed, spins, table)
+    )(dirs, packed, minus, plus, table)
 
 
 def sum_over_space(partial, ranks):
     rows, width = partial.shape
-    pieces = lax.all_to_all(partial.reshape(ranks, rows // ranks, width), "space", 0, 0, tiled=True)
-    total = jnp.sum(pieces.astype(F32), axis=0).astype(BF16)
-    spread_out = jnp.broadcast_to(total[None], (ranks,) + total.shape)
-    whole = lax.all_to_all(spread_out, "space", 0, 0, tiled=True)
+    near = 4 if ranks % 4 == 0 else 2
+    groups = [list(range(first, first + near)) for first in range(0, ranks, near)]
+    pieces = lax.all_to_all(
+        partial.reshape(near, rows // near, width),
+        "space",
+        0,
+        0,
+        axis_index_groups=groups,
+        tiled=True,
+    )
+    total = jnp.sum(pieces.astype(F32), axis=0)
+    stride = near
+    while stride < ranks:
+        other = lax.ppermute(total.astype(BF16), "space", [(i, i ^ stride) for i in range(ranks)])
+        total = total + other.astype(F32)
+        stride *= 2
+    whole = jnp.broadcast_to(total.astype(BF16)[None], (near,) + total.shape)
+    whole = lax.all_to_all(whole, "space", 0, 0, axis_index_groups=groups, tiled=True)
     return whole.reshape(rows, width)
 
 
@@ -237,17 +257,22 @@
     vectors, sites = eigvecs.shape[2], eigvecs.shape[4]
     assert sites == LX * LZ and ranks % 2 == 0
     field = jnp.transpose(eigvecs[0], (0, 2, 3, 1)).reshape(6 * sites, vectors)
-    link_rows = links[0].reshape(54, sites)
+    link_rows = links[0].reshape(27, 2, sites)
     half = half_rows(sites)
     rows = 6 * half + padded(18)
 
-    payload = jax.ShapeDtypeStruct((rows, vectors), BF16)
+    payload = pltpu.VMEM((rows, vectors), BF16)
     across, along = pl.pallas_call(
         functools.partial(prepare_kernel, sites),
         out_shape=(payload, payload),
-        in_specs=[VMEM] * 2,
+        in_specs=[HBM, HBM],
         out_specs=(VMEM, VMEM),
-        compiler_params=PARAMS,
+        scratch_shapes=[
+            pltpu.VMEM((9, 2, sites), BF16),
+            pltpu.SemaphoreType.DMA((2, 6)),
+            pltpu.SemaphoreType.DMA,
+        ],
+        compiler_params=pltpu.CompilerParams(vmem_limit_bytes=VMEM_BYTES - 4 * rows * vectors),
     )(field, link_rows)
     from_across = lax.ppermute(across, "space", [(i, i ^ 1) for i in range(ranks)])
     from_along = lax.ppermute(
@@ -267,14 +292,15 @@
         compiler_params=PARAMS,
     )(field, link_rows)
     columns = partner.shape[1]
-    spins, table = pl.pallas_call(
+    minus, plus, table = pl.pallas_call(
         spins_kernel,
         out_shape=(
-            jax.ShapeDtypeStruct((SPIN * columns, 2 * vectors), BF16),
+            jax.ShapeDtypeStruct((2 * SPIN * columns, vectors), BF16),
+            jax.ShapeDtypeStruct((2 * SPIN * columns, vectors), BF16),
             jax.ShapeDtypeStruct((SPIN * 128, SPIN * 128), BF16),
         ),
         in_specs=[VMEM],
-        out_specs=(VMEM, VMEM),
+        out_specs=(VMEM, VMEM, VMEM),
         cost_estimate=pl.CostEstimate(flops=500_000_000, bytes_accessed=2_000_000, transcendentals=0),
         compiler_params=PARAMS,
     )(partner)
@@ -296,7 +322,7 @@
     )(along, from_across, from_along, packed)
     packed = sum_over_space(packed, ranks)
     shape = (dirs.shape[0], 2, columns, SPIN * vectors)
-    result = last_call(dirs, packed, spins, table, shape)
+    result = last_call(dirs, packed, minus, plus, table, shape)
     return result[None]
 
 

time: 54.2 us -> 49.5 us (0.913)
  blocking collectives: 16.4 us -> 8.95 us
  starting transfers between devices: 10.1 us -> 14.3 us
  waiting for transfers between devices: 14.1 us -> 10.5 us
  Pallas kernels: 10.4 us -> 12.6 us
    all_to_all x1, blocking collectives: 16.4 us -> 8.95 us  [sum_over_space(): lax.all_to_all(partial.reshape(near, rows // near, width), 'space', 0, 0,...]
    all_to_all x1, waiting for transfers between devices: 8.09 us -> 2.87 us  [sum_over_space(): lax.all_to_all(whole, 'space', 0, 0, axis_index_groups=groups, tiled=True)]
    ppermute x0 -> x1, starting transfers between devices: none -> 4.11 us  [sum_over_space(): lax.ppermute(total.astype(BF16), 'space', [(i, i ^ stride) for i in range...]
    ppermute x0 -> x1, waiting for transfers between devices: none -> 3.47 us  [sum_over_space(): lax.ppermute(total.astype(BF16), 'space', [(i, i ^ stride) for i in range...]
    ppermute x1, waiting for transfers between devices: 1.55 us -> 0.01 us  [blocks(): lax.ppermute(across, 'space', [(i, i ^ 1) for i in range(ranks)])]
    pallas_call x1, Pallas kernels: 0.08 us -> 1.23 us  [blocks(): pl.pallas_call(functools.partial(prepare_kernel, sites), out_shape=(paylo...]
    pallas_call x1, Pallas kernels: 4.16 us -> 5.09 us  [last_call(): pl.pallas_call(last_kernel, grid_spec=pltpu.PrefetchScalarGridSpec(num_sc...]
    another operation x1 -> x0, local copies, waits for them, and re-layouts: 0.79 us -> none  [blocks(): link_rows = links[0].reshape(54, sites)]
  transfers between devices with their start and end apart: 4 -> 5, of which waited for: 4 -> 4; matrix products, arithmetic and copies ran while one was open for 0% -> 0% of each run, Pallas kernels for 8% -> 8%
where the time goes in v3:
time: 49.5 us; the launch traced here: 49.1 us
  starting transfers between devices  14.3 us (29%)
  Pallas kernels  12.6 us (25%)
  waiting for transfers between devices  10.5 us (21%)
  blocking collectives  8.95 us (18%)
  local copies, waits for them, and re-layouts  2.62 us (5%)
    all_to_all x1, blocking collectives, sum_over_space(): lax.all_to_all(partial.reshape(near, rows // near, width), 'space', 0, 0,...  8.95 us
    pallas_call x1, Pallas kernels, last_call(): pl.pallas_call(last_kernel, grid_spec=pltpu.PrefetchScalarGridSpec(num_sc...  5.09 us
    ppermute x1, starting transfers between devices, sum_over_space(): lax.ppermute(total.astype(BF16), 'space', [(i, i ^ stride) for i in range...  4.11 us
    ppermute x1, starting transfers between devices, blocks(): lax.ppermute(along, 'space', [((i + 2) % ranks if i % 2 == 0 else (i - 2)...  3.6 us
    ppermute x1, waiting for transfers between devices, sum_over_space(): lax.ppermute(total.astype(BF16), 'space', [(i, i ^ stride) for i in range...  3.47 us
    all_to_all x1, starting transfers between devices, sum_over_space(): lax.all_to_all(whole, 'space', 0, 0, axis_index_groups=groups, tiled=True)  3.46 us
    pallas_call x1, Pallas kernels, blocks(): pl.pallas_call(functools.partial(front_kernel, sites), out_shape=jax.Shap...  3.18 us
    ppermute x1, starting transfers between devices, blocks(): lax.ppermute(across, 'space', [(i, i ^ 1) for i in range(ranks)])  3.03 us
  transfers between devices with their start and end apart: 5, of which 4 were waited for; matrix products, arithmetic and copies ran while one was open for 0% of the time, Pallas kernels for 8%

profile of v3, /device:TPU:0, one launch (start us, length us, event | category | flops | bytes accessed | tf_op | source)
XLA Modules:
  0.0 49.1 jit_solution(9706763532730615)
XLA Ops:
  0.0 1.2 %shard_map.46 = (bf16[696,256]{1,0:T(8,128)(2,1)S(1)}, bf16[696,256]{1,0:T(8,128)(2,1)S(1)}) custom-call(bf16[1296,256]{1,0:T(8,128)(2,1)} %bitcast.11, bf16[27,2,216]{2,1,0:T(2,128)(2,1)} %bitcast.14), custom_call_target="tpu_custom_call" | custom-call | tf_op jit(solution)/shard_map/pallas_call | solution.py:265
  1.2 3.0 %collective-permute-start = (bf16[696,256]{1,0:T(8,128)(2,1)S(1)}, bf16[696,256]{1,0:T(8,128)(2,1)S(1)}, u32[]{:S(2)}, u32[]{:S(2)}) collective-permute-start(bf16[696,256]{1,0:T(8,128)(2,1)S(1)} %get-tuple-element.11), channel_id=1, source_target_pairs={{0,2},{2,0},{4,6},{6,4},{8,10},{10,8},{12,14},{14,12},{1,3},{3,1},... | collective-permute-start | bytes 1069064 | tf_op jit(solution)/shard_map/ppermute | solution.py:277
  4.3 3.6 %collective-permute-start.1 = (bf16[696,256]{1,0:T(8,128)(2,1)S(1)}, bf16[696,256]{1,0:T(8,128)(2,1)S(1)}, u32[]{:S(2)}, u32[]{:S(2)}) collective-permute-start(bf16[696,256]{1,0:T(8,128)(2,1)S(1)} %get-tuple-element.10.own_ref), channel_id=1, source_target_pairs={{4,0},{14,2},{8,4},{2,6},{12,8},{6,10},{0,12},{10,14},{5,1},{15,3}... | collective-permute-start | bytes 1069064 | tf_op jit(solution)/shard_map/ppermute | solution.py:278
  7.9 0.0 copy-start
  7.9 1.1 %copy-done = bf16[1,2,256,3,216]{2,4,3,1,0:T(8,128)(2,1)S(1)} copy-done((bf16[1,2,256,3,216]{2,4,3,1,0:T(8,128)(2,1)S(1)}, bf16[1,2,256,3,216]{2,4,3,1,0:T(8,128)(2,1)}, u32[]{:S(2)}) %copy-start) | copy-done | bytes 663576
  9.0 0.7 %copy-done.1 = bf16[1,3,3,3,2,216]{5,4,3,2,1,0:T(2,128)(2,1)S(1)} copy-done((bf16[1,3,3,3,2,216]{5,4,3,2,1,0:T(2,128)(2,1)S(1)}, bf16[1,3,3,3,2,216]{5,4,3,2,1,0:T(2,128)(2,1)}, u32[]{:S(2)}) %copy-start.1) | copy-done | bytes 23352
  9.7 3.2 %shard_map.47.flat_ref = bf16[768,256]{1,0:T(8,128)(2,1)S(1)} custom-call(bf16[1296,256]{1,0:T(8,128)(2,1)S(1)} %bitcast.12, bf16[27,2,216]{2,1,0:T(2,128)(2,1)S(1)} %bitcast.15), custom_call_target="tpu_custom_call" | custom-call | flops 700000000 | bytes 8000000 | tf_op jit(solution)/shard_map/pallas_call | solution.py:285
  12.9 0.0 collective-permute-done.across_ref
  12.9 2.3 %collective-permute-done.1.along_ref = bf16[696,256]{1,0:T(8,128)(2,1)S(1)} collective-permute-done((bf16[696,256]{1,0:T(8,128)(2,1)S(1)}, bf16[696,256]{1,0:T(8,128)(2,1)S(1)}, u32[]{:S(2)}, u32[]{:S(2)}) %collective-permute-start.1) | collective-permute-done | bytes 356384 | tf_op jit(solution)/shard_map/ppermute | solution.py:278
  15.2 2.1 %shard_map.48 = bf16[768,256]{1,0:T(8,128)(2,1)S(1)} custom-call(bf16[696,256]{1,0:T(8,128)(2,1)S(1)} %get-tuple-element.10.own_ref, bf16[696,256]{1,0:T(8,128)(2,1)S(1)} %collective-permute-done.across_ref, bf16[696,256]{1,0:T(8,128)(2,1)S(1)} %collective-permute-done.1.along_ref, ...), custom_call_target="tpu_custom_call", output_to_operand_aliasing={{}: (3, {})} | custom-call | flops 400000000 | bytes 4000000 | tf_op jit(solution)/shard_map/pallas_call | solution.py:307
  17.3 0.0 copy-start.3
  17.3 9.0 %all_to_all.10 = bf16[4,192,256]{2,1,0:T(8,128)(2,1)S(1)} all-to-all(bf16[4,192,256]{2,1,0:T(8,128)(2,1)S(1)} %bitcast.10), channel_id=1, replica_groups={{0,2,4,6},{8,10,12,14},{1,3,5,7},{9,11,13,15},{16,18,20,22},{24,26,28,3..., dimensions={0} | all-to-all | bytes 786432 | tf_op jit(solution)/shard_map/all_to_all | solution.py:236
  26.3 4.1 %collective-permute-start.2 = (bf16[192,256]{1,0:T(8,128)(2,1)S(1)}, bf16[192,256]{1,0:T(8,128)(2,1)S(1)}, u32[]{:S(2)}, u32[]{:S(2)}) collective-permute-start(bf16[192,256]{1,0:T(8,128)(2,1)S(1)} %convert_element_type.13), channel_id=1, source_target_pairs={{0,8},{2,10},{4,12},{6,14},{8,0},{10,2},{12,4},{14,6},{1,9},{3,11}... | collective-permute-start | bytes 294920 | tf_op jit(solution)/shard_map/ppermute | solution.py:247
  30.4 3.5 %collective-permute-done.2 = bf16[192,256]{1,0:T(8,128)(2,1)S(1)} collective-permute-done((bf16[192,256]{1,0:T(8,128)(2,1)S(1)}, bf16[192,256]{1,0:T(8,128)(2,1)S(1)}, u32[]{:S(2)}, u32[]{:S(2)}) %collective-permute-start.2) | collective-permute-done | bytes 98336 | tf_op jit(solution)/shard_map/ppermute | solution.py:247
  33.9 0.0 copy-start.2
  33.9 0.8 %broadcast_in_dim.4 = bf16[4,192,256]{2,1,0:T(8,128)(2,1)} broadcast(bf16[192,256]{1,0:T(8,128)(2,1)S(1)} %add_convert_fusion), dimensions={1,2} | broadcast | bytes 491520 | tf_op jit(solution)/shard_map/broadcast_in_dim | solution.py:250
  34.7 3.5 %all-to-all-start.1 = ((bf16[4,192,256]{2,1,0:T(8,128)(2,1)}), bf16[4,192,256]{2,1,0:T(8,128)(2,1)S(1)}, u32[]{:S(2)}, u32[]{:S(2)}) async-start(bf16[4,192,256]{2,1,0:T(8,128)(2,1)} %broadcast_in_dim.4), calls=%async_computation.1 | async-start | bytes 786432 | tf_op jit(solution)/shard_map/all_to_all | solution.py:251
  38.2 0.0 copy-done.3
  38.2 0.1 collective-permute-start.3
  38.3 1.9 %collective-permute-done.3.p_ref = bf16[2,128,1024]{2,1,0:T(8,128)(2,1)S(1)} collective-permute-done((bf16[2,128,1024]{2,1,0:T(8,128)(2,1)S(1)}, bf16[2,128,1024]{2,1,0:T(8,128)(2,1)S(1)}, u32[]{:S(2)}, u32[]{:S(2)}) %collective-permute-start.3) | collective-permute-done | bytes 524320 | tf_op jit(solution)/shard_map/ppermute | solution.py:283
  40.2 1.0 %shard_map.49 = (bf16[1024,256]{1,0:T(8,128)(2,1)S(1)}, bf16[1024,256]{1,0:T(8,128)(2,1)S(1)}, bf16[512,512]{1,0:T(8,128)(2,1)S(1)}) custom-call(bf16[2,128,1024]{2,1,0:T(8,128)(2,1)S(1)} %collective-permute-done.3.p_ref), custom_call_target="tpu_custom_call" | custom-call | flops 500000000 | bytes 2000000 | tf_op jit(solution)/shard_map/pallas_call | solution.py:295
  41.1 2.9 %all-to-all-done.1 = bf16[4,192,256]{2,1,0:T(8,128)(2,1)S(1)} async-done(((bf16[4,192,256]{2,1,0:T(8,128)(2,1)}), bf16[4,192,256]{2,1,0:T(8,128)(2,1)S(1)}, u32[]{:S(2)}, u32[]{:S(2)}) %all-to-all-start.1) | async-done | bytes 393248 | tf_op jit(solution)/shard_map/all_to_all | solution.py:251
  44.0 0.0 copy-done.2
  44.0 5.1 %shard_map.50 = bf16[3,2,128,1024]{3,2,1,0:T(8,128)(2,1)} custom-call(s32[3]{0:T(128)S(1)} %copy-done.2, bf16[768,256]{1,0:T(8,128)(2,1)S(1)} %bitcast.13, bf16[1024,256]{1,0:T(8,128)(2,1)S(1)} %get-tuple-element.12.minus_ref, bf16[1024,256]{1,0:T(8,128)(2,1)S(1)} %get-tuple-element.13.plus_ref, bf16[512,512]{1,0:T(8,128)(2,1)S(1)} %get-tuple-element.14.s_ref), custom_call_target="tpu_custom_call" | custom-call | flops 2400000000 | bytes 3000000 | tf_op jit(solution)/shard_map/pallas_call | solution.py:211
  (4 shorter events, 0.1 us)
Async XLA Ops:
  1.2 11.7 %collective-permute-start = (bf16[696,256]{1,0:T(8,128)(2,1)S(1)}, bf16[696,256]{1,0:T(8,128)(2,1)S(1)}, u32[]{:S(2)}, u32[]{:S(2)}) collective-permute-start(bf16[696,256]{1,0:T(8,128)(2,1)S(1)} %get-tuple-element.11), channel_id=1, source_target_pairs={{0,2},{2,0},{4,6},{6,4},{8,10},{10,8},{12,14},{14,12},{1,3},{3,1},... | collective-permute-start | bytes 1069064 | tf_op jit(solution)/shard_map/ppermute | solution.py:277
  4.3 10.9 %collective-permute-start.1 = (bf16[696,256]{1,0:T(8,128)(2,1)S(1)}, bf16[696,256]{1,0:T(8,128)(2,1)S(1)}, u32[]{:S(2)}, u32[]{:S(2)}) collective-permute-start(bf16[696,256]{1,0:T(8,128)(2,1)S(1)} %get-tuple-element.10.own_ref), channel_id=1, source_target_pairs={{4,0},{14,2},{8,4},{2,6},{12,8},{6,10},{0,12},{10,14},{5,1},{15,3}... | collective-permute-start | bytes 1069064 | tf_op jit(solution)/shard_map/ppermute | solution.py:278
  7.9 1.1 %copy-start = (bf16[1,2,256,3,216]{2,4,3,1,0:T(8,128)(2,1)S(1)}, bf16[1,2,256,3,216]{2,4,3,1,0:T(8,128)(2,1)}, u32[]{:S(2)}) copy-start(bf16[1,2,256,3,216]{2,4,3,1,0:T(8,128)(2,1)} %param.4) | copy-start | bytes 1990660
  9.0 0.7 %copy-start.1 = (bf16[1,3,3,3,2,216]{5,4,3,2,1,0:T(2,128)(2,1)S(1)}, bf16[1,3,3,3,2,216]{5,4,3,2,1,0:T(2,128)(2,1)}, u32[]{:S(2)}) copy-start(bf16[1,3,3,3,2,216]{5,4,3,2,1,0:T(2,128)(2,1)} %param.5) | copy-start | bytes 69988
  17.3 20.9 %copy-start.3 = (bf16[1,2,128,1024]{3,2,1,0:T(8,128)(2,1)S(1)}, bf16[1,2,128,1024]{3,2,1,0:T(8,128)(2,1)}, u32[]{:S(2)}) copy-start(bf16[1,2,128,1024]{3,2,1,0:T(8,128)(2,1)} %param.7) | copy-start | bytes 1572868
  26.3 7.6 %collective-permute-start.2 = (bf16[192,256]{1,0:T(8,128)(2,1)S(1)}, bf16[192,256]{1,0:T(8,128)(2,1)S(1)}, u32[]{:S(2)}, u32[]{:S(2)}) collective-permute-start(bf16[192,256]{1,0:T(8,128)(2,1)S(1)} %convert_element_type.13), channel_id=1, source_target_pairs={{0,8},{2,10},{4,12},{6,14},{8,0},{10,2},{12,4},{14,6},{1,9},{3,11}... | collective-permute-start | bytes 294920 | tf_op jit(solution)/shard_map/ppermute | solution.py:247
  33.9 10.1 %copy-start.2 = (s32[3]{0:T(128)S(1)}, s32[3]{0:T(128)}, u32[]{:S(2)}) copy-start(s32[3]{0:T(128)} %places_ref.1) | copy-start | bytes 40
  34.7 9.3 %all-to-all-start.1 = ((bf16[4,192,256]{2,1,0:T(8,128)(2,1)}), bf16[4,192,256]{2,1,0:T(8,128)(2,1)S(1)}, u32[]{:S(2)}, u32[]{:S(2)}) async-start(bf16[4,192,256]{2,1,0:T(8,128)(2,1)} %broadcast_in_dim.4), calls=%async_computation.1 | async-start | bytes 786432 | tf_op jit(solution)/shard_map/all_to_all | solution.py:251
  38.2 2.0 %collective-permute-start.3 = (bf16[2,128,1024]{2,1,0:T(8,128)(2,1)S(1)}, bf16[2,128,1024]{2,1,0:T(8,128)(2,1)S(1)}, u32[]{:S(2)}, u32[]{:S(2)}) collective-permute-start(bf16[2,128,1024]{2,1,0:T(8,128)(2,1)S(1)} %bitcast.16), channel_id=1, source_target_pairs={{1,0},{0,1},{3,2},{2,3},{5,4},{4,5},{7,6},{6,7},{9,8},{8,9},{11,10... | collective-permute-start | bytes 1572872 | tf_op jit(solution)/shard_map/ppermute | solution.py:283

commit v4 on v3

--- a/solution.py
+++ b/solution.py
@@ -127,27 +127,32 @@
         o_ref[pl.ds(index * vectors, vectors), :] = packed.astype(BF16)
 
 
-def middle_kernel(half, own_ref, across_ref, along_ref, flat_ref, o_ref, w_ref, pack_ref, sem):
+def pair_product(half, left_ref, right_ref, w_ref):
     even = lax.rem(lax.axis_index("space"), 2) == 0
-    first = jnp.where(even, own_ref[...], along_ref[...])
-    last = jnp.where(even, along_ref[...], own_ref[...])
-    middle = across_ref[...]
-    ident = identity(half)
-    for index, field in enumerate((first, middle)):
-        columns = dot(ident, field[6 * half :, :half], 1, 1)
-        vec = [field[comp * half : (comp + 1) * half, :].astype(F32) for comp in range(6)]
-        for comp, value in enumerate(adjoint_product(columns, 0, vec)):
-            part, inner = comp // 3, comp % 3
-            w_ref[part, pl.ds((index * 3 + inner) * half, half), :] = value
-    v_real = jnp.concatenate([middle[: 3 * half], last[: 3 * half]], axis=0)
-    v_imag = jnp.concatenate([middle[3 * half : 6 * half], last[3 * half : 6 * half]], axis=0)
-    packed = packed_elemental(w_ref[0].astype(BF16), w_ref[1].astype(BF16), v_real, v_imag)
-    del flat_ref
-    pack_ref[...] = packed.astype(BF16)
-    vectors = packed.shape[0]
-    copy = pltpu.make_async_copy(pack_ref, o_ref.at[pl.ds(2 * vectors, vectors)], sem)
-    copy.start()
-    copy.wait()
+    left, right = left_ref[...], right_ref[...]
+    field = jnp.where(even, left, right)
+    ahead = jnp.where(even, right, left)
+    columns = dot(identity(half), field[6 * half :, :half], 1, 1)
+    vec = [field[comp * half : (comp + 1) * half, :].astype(F32) for comp in range(6)]
+    for comp, value in enumerate(adjoint_product(columns, 0, vec)):
+        w_ref[pl.ds(comp * half, half), :] = value
+    return packed_elemental(
+        w_ref[pl.ds(0, 3 * half), :].astype(BF16),
+        w_ref[pl.ds(3 * half, 3 * half), :].astype(BF16),
+        ahead[: 3 * half],
+        ahead[3 * half : 6 * half],
+    )
+
+
+def first_pair_kernel(half, own_ref, across_ref, o_ref, w_ref):
+    o_ref[...] = pair_product(half, own_ref, across_ref, w_ref)
+
+
+def second_pair_kernel(half, across_ref, along_ref, flat_ref, first_ref, o_ref, w_ref):
+    done = flat_ref.shape[0]
+    o_ref[pl.ds(0, done), :] = flat_ref[...]
+    packed = first_ref[...] + pair_product(half, across_ref, along_ref, w_ref)
+    o_ref[pl.ds(done, packed.shape[0]), :] = packed.astype(BF16)
 
 
 def spread(size):
@@ -180,48 +185,56 @@
             plus_ref[below, to] = less[:, lanes]
 
 
-def last_kernel(places_ref, m_ref, minus_ref, plus_ref, s_ref, o_ref):
+def last_kernel(dirs_ref, m_ref, minus_ref, plus_ref, s_ref, o_ref, product_ref, whole_ref, sems):
+    vectors = m_ref.shape[1]
     columns = o_ref.shape[2]
-    vectors = m_ref.shape[1]
     block = s_ref.shape[0] // SPIN
-    packed = m_ref[...]
-    product = (dot(minus_ref[...], packed, 1, 1) + dot(plus_ref[...], packed, 1, 0)).astype(BF16)
-    for chunk in range(vectors // block):
-        at = chunk * block
-        piece = jnp.concatenate(
-            [
-                product[2 * spin * columns : 2 * (spin + 1) * columns, at : at + block]
-                for spin in range(SPIN)
-            ],
-            axis=1,
-        )
-        apart = dot(piece, s_ref[...], 1, 0).astype(BF16)
-        to = pl.ds(at * SPIN, block * SPIN)
-        o_ref[0, 0, :, to] = apart[:columns]
-        o_ref[0, 1, :, to] = apart[columns:]
+    copies = []
+    for index, direction in enumerate((0, 2, 1)):
+        packed = m_ref[pl.ds(index * vectors, vectors), :]
+        for spin in range(SPIN):
+            rows = pl.ds(2 * spin * columns, 2 * columns)
+            product_ref[index % 2, rows, :] = (
+                dot(minus_ref[rows, :], packed, 1, 1) + dot(plus_ref[rows, :], packed, 1, 0)
+            ).astype(BF16)
+        place = jnp.where(dirs_ref[1] == direction, 1, jnp.where(dirs_ref[2] == direction, 2, 0))
+        for chunk in range(vectors // block):
+            piece = jnp.concatenate(
+                [
+                    product_ref[
+                        index % 2,
+                        pl.ds(2 * spin * columns, 2 * columns),
+                        pl.ds(chunk * block, block),
+                    ]
+                    for spin in range(SPIN)
+                ],
+                axis=1,
+            )
+            apart = dot(piece, s_ref[...], 1, 0).astype(BF16)
+            to = pl.ds(chunk * block * SPIN, block * SPIN)
+            whole_ref[index, 0, :, to] = apart[:columns]
+            whole_ref[index, 1, :, to] = apart[columns:]
+            copy = pltpu.make_async_copy(
+                whole_ref.at[index, :, :, to], o_ref.at[place, :, :, to], sems.at[index, chunk]
+            )
+            copy.start()
+            copies.append(copy)
+    for copy in copies:
+        copy.wait()
 
 
 def last_call(dirs, packed, minus, plus, table, shape):
     vectors = packed.shape[1]
-
-    def place(direction, dirs_ref):
-        at = jnp.where(dirs_ref[1] == direction, 1, jnp.where(dirs_ref[2] == direction, 2, 0))
-        return at, 0, 0, 0
-
     return pl.pallas_call(
         last_kernel,
-        grid_spec=pltpu.PrefetchScalarGridSpec(
-            num_scalar_prefetch=1,
-            grid=(shape[0],),
-            in_specs=[
-                pl.BlockSpec((vectors, vectors), lambda i, at: (lax.rem(2 * i, 3), 0)),
-                VMEM,
-                VMEM,
-                VMEM,
-            ],
-            out_specs=pl.BlockSpec((1,) + shape[1:], place),
-        ),
+        in_specs=[pl.BlockSpec(memory_space=pltpu.SMEM)] + [VMEM] * 4,
+        out_specs=HBM,
         out_shape=jax.ShapeDtypeStruct(shape, BF16),
+        scratch_shapes=[
+            pltpu.VMEM((2,) + minus.shape, BF16),
+            pltpu.VMEM(shape, BF16),
+            pltpu.SemaphoreType.DMA((shape[0], vectors * SPIN // table.shape[0])),
+        ],
         cost_estimate=pl.CostEstimate(
             flops=2_400_000_000, bytes_accessed=3_000_000, transcendentals=0
         ),
@@ -282,9 +295,9 @@
     )
     partner = lax.ppermute(peram[0], "tm", [((i + 1) % 2, i) for i in range(2)])
 
-    packed = pl.pallas_call(
+    flat = pl.pallas_call(
         functools.partial(front_kernel, sites),
-        out_shape=jax.ShapeDtypeStruct((3 * vectors, vectors), BF16),
+        out_shape=jax.ShapeDtypeStruct((2 * vectors, vectors), BF16),
         in_specs=[VMEM] * 2,
         out_specs=VMEM,
         scratch_shapes=[pltpu.VMEM((2, 6 * sites, vectors), F32)],
@@ -304,22 +317,26 @@
         cost_estimate=pl.CostEstimate(flops=500_000_000, bytes_accessed=2_000_000, transcendentals=0),
         compiler_params=PARAMS,
     )(partner)
+    pair_cost = pl.CostEstimate(flops=200_000_000, bytes_accessed=2_000_000, transcendentals=0)
+    pair_scratch = [pltpu.VMEM((6 * half, vectors), F32)]
+    upright = pl.pallas_call(
+        functools.partial(first_pair_kernel, half),
+        out_shape=jax.ShapeDtypeStruct((vectors, vectors), F32),
+        in_specs=[VMEM] * 2,
+        out_specs=VMEM,
+        scratch_shapes=pair_scratch,
+        cost_estimate=pair_cost,
+        compiler_params=PARAMS,
+    )(along, from_across)
     packed = pl.pallas_call(
-        functools.partial(middle_kernel, half),
+        functools.partial(second_pair_kernel, half),
         out_shape=jax.ShapeDtypeStruct((3 * vectors, vectors), BF16),
-        in_specs=[VMEM] * 3 + [ANY],
-        out_specs=ANY,
-        scratch_shapes=[
-            pltpu.VMEM((2, 6 * half, vectors), F32),
-            pltpu.VMEM((vectors, vectors), BF16),
-            pltpu.SemaphoreType.DMA,
-        ],
-        input_output_aliases={3: 0},
-        cost_estimate=pl.CostEstimate(
-            flops=400_000_000, bytes_accessed=4_000_000, transcendentals=0
-        ),
-        compiler_params=PARAMS,
-    )(along, from_across, from_along, packed)
+        in_specs=[VMEM] * 4,
+        out_specs=VMEM,
+        scratch_shapes=pair_scratch,
+        cost_estimate=pair_cost,
+        compiler_params=PARAMS,
+    )(from_across, from_along, flat, upright)
     packed = sum_over_space(packed, ranks)
     shape = (dirs.shape[0], 2, columns, SPIN * vectors)
     result = last_call(dirs, packed, minus, plus, table, shape)

time: 49.5 us -> 46.7 us (0.943)
  Pallas kernels: 12.6 us -> 11 us
  waiting for transfers between devices: 10.5 us -> 9.3 us
    pallas_call x2 -> x3, Pallas kernels: 7.19 us -> 5.59 us  [the longest x1 3.18 us: last_call(): pl.pallas_call(last_kernel, in_specs=[pl.BlockSpec(memory_space=pltpu.SME...]
    ppermute x1, waiting for transfers between devices: 2.26 us -> 1.05 us  [blocks(): lax.ppermute(along, 'space', [((i + 2) % ranks if i % 2 == 0 else (i - 2)...]
  transfers between devices with their start and end apart: 5 -> 5, of which waited for: 4 -> 4; matrix products, arithmetic and copies ran while one was open for 0% -> 0% of each run, Pallas kernels for 8% -> 12%
where the time goes in v4:
time: 46.7 us; the launch traced here: 46.3 us
  starting transfers between devices  14.2 us (30%)
  Pallas kernels  11 us (24%)
  waiting for transfers between devices  9.3 us (20%)
  blocking collectives  9.02 us (19%)
  local copies, waits for them, and re-layouts  2.62 us (6%)
    all_to_all x1, blocking collectives, sum_over_space(): lax.all_to_all(partial.reshape(near, rows // near, width), 'space', 0, 0,...  9.02 us
    ppermute x1, starting transfers between devices, sum_over_space(): lax.ppermute(total.astype(BF16), 'space', [(i, i ^ stride) for i in range...  4.04 us
    ppermute x1, starting transfers between devices, blocks(): lax.ppermute(along, 'space', [((i + 2) % ranks if i % 2 == 0 else (i - 2)...  3.6 us
    ppermute x1, waiting for transfers between devices, sum_over_space(): lax.ppermute(total.astype(BF16), 'space', [(i, i ^ stride) for i in range...  3.47 us
    all_to_all x1, starting transfers between devices, sum_over_space(): lax.all_to_all(whole, 'space', 0, 0, axis_index_groups=groups, tiled=True)  3.46 us
    pallas_call x1, Pallas kernels, blocks(): pl.pallas_call(functools.partial(front_kernel, sites), out_shape=jax.Shap...  3.18 us
    pallas_call x1, Pallas kernels, last_call(): pl.pallas_call(last_kernel, in_specs=[pl.BlockSpec(memory_space=pltpu.SME...  3.18 us
    ppermute x1, starting transfers between devices, blocks(): lax.ppermute(across, 'space', [(i, i ^ 1) for i in range(ranks)])  3.03 us
  transfers between devices with their start and end apart: 5, of which 4 were waited for; matrix products, arithmetic and copies ran while one was open for 0% of the time, Pallas kernels for 12%

profile of v4, /device:TPU:0, one launch (start us, length us, event | category | flops | bytes accessed | tf_op | source)
XLA Modules:
  0.0 46.3 jit_solution(8535754422583653826)
XLA Ops:
  0.0 1.2 %shard_map.46 = (bf16[696,256]{1,0:T(8,128)(2,1)S(1)}, bf16[696,256]{1,0:T(8,128)(2,1)S(1)}) custom-call(bf16[1296,256]{1,0:T(8,128)(2,1)} %bitcast.11, bf16[27,2,216]{2,1,0:T(2,128)(2,1)} %bitcast.14), custom_call_target="tpu_custom_call" | custom-call | tf_op jit(solution)/shard_map/pallas_call | solution.py:278
  1.2 3.0 %collective-permute-start = (bf16[696,256]{1,0:T(8,128)(2,1)S(1)}, bf16[696,256]{1,0:T(8,128)(2,1)S(1)}, u32[]{:S(2)}, u32[]{:S(2)}) collective-permute-start(bf16[696,256]{1,0:T(8,128)(2,1)S(1)} %get-tuple-element.10), channel_id=1, source_target_pairs={{0,2},{2,0},{4,6},{6,4},{8,10},{10,8},{12,14},{14,12},{1,3},{3,1},... | collective-permute-start | bytes 1069064 | tf_op jit(solution)/shard_map/ppermute | solution.py:290
  4.3 3.6 %collective-permute-start.1 = (bf16[696,256]{1,0:T(8,128)(2,1)S(1)}, bf16[696,256]{1,0:T(8,128)(2,1)S(1)}, u32[]{:S(2)}, u32[]{:S(2)}) collective-permute-start(bf16[696,256]{1,0:T(8,128)(2,1)S(1)} %get-tuple-element.11.own_ref), channel_id=1, source_target_pairs={{4,0},{14,2},{8,4},{2,6},{12,8},{6,10},{0,12},{10,14},{5,1},{15,3}... | collective-permute-start | bytes 1069064 | tf_op jit(solution)/shard_map/ppermute | solution.py:291
  7.9 1.1 %copy-done = bf16[1,2,256,3,216]{2,4,3,1,0:T(8,128)(2,1)S(1)} copy-done((bf16[1,2,256,3,216]{2,4,3,1,0:T(8,128)(2,1)S(1)}, bf16[1,2,256,3,216]{2,4,3,1,0:T(8,128)(2,1)}, u32[]{:S(2)}) %copy-start) | copy-done | bytes 663576
  9.0 0.7 %copy-done.1 = bf16[1,3,3,3,2,216]{5,4,3,2,1,0:T(2,128)(2,1)S(1)} copy-done((bf16[1,3,3,3,2,216]{5,4,3,2,1,0:T(2,128)(2,1)S(1)}, bf16[1,3,3,3,2,216]{5,4,3,2,1,0:T(2,128)(2,1)}, u32[]{:S(2)}) %copy-start.1) | copy-done | bytes 23352
  9.7 3.2 %shard_map.47.flat_ref = bf16[512,256]{1,0:T(8,128)(2,1)S(1)} custom-call(bf16[1296,256]{1,0:T(8,128)(2,1)S(1)} %bitcast.12, bf16[27,2,216]{2,1,0:T(2,128)(2,1)S(1)} %bitcast.15), custom_call_target="tpu_custom_call" | custom-call | flops 700000000 | bytes 8000000 | tf_op jit(solution)/shard_map/pallas_call | solution.py:298
  12.9 0.0 collective-permute-done.across_ref
  12.9 1.2 %shard_map.48.first_ref = f32[256,256]{1,0:T(8,128)S(1)} custom-call(bf16[696,256]{1,0:T(8,128)(2,1)S(1)} %get-tuple-element.11.own_ref, bf16[696,256]{1,0:T(8,128)(2,1)S(1)} %collective-permute-done.across_ref), custom_call_target="tpu_custom_call" | custom-call | flops 200000000 | bytes 2000000 | tf_op jit(solution)/shard_map/pallas_call | solution.py:322
  14.1 1.0 %collective-permute-done.1.along_ref = bf16[696,256]{1,0:T(8,128)(2,1)S(1)} collective-permute-done((bf16[696,256]{1,0:T(8,128)(2,1)S(1)}, bf16[696,256]{1,0:T(8,128)(2,1)S(1)}, u32[]{:S(2)}, u32[]{:S(2)}) %collective-permute-start.1) | collective-permute-done | bytes 356384 | tf_op jit(solution)/shard_map/ppermute | solution.py:291
  15.2 1.2 %shard_map.49 = bf16[768,256]{1,0:T(8,128)(2,1)S(1)} custom-call(bf16[696,256]{1,0:T(8,128)(2,1)S(1)} %collective-permute-done.across_ref, bf16[696,256]{1,0:T(8,128)(2,1)S(1)} %collective-permute-done.1.along_ref, bf16[512,256]{1,0:T(8,128)(2,1)S(1)} %shard_map.47.flat_ref, f32[256,256]{1,0:T(8,128)S(1)} %shard_map.48.first_ref), custom_call_target="tpu_custom_call" | custom-call | flops 200000000 | bytes 2000000 | tf_op jit(solution)/shard_map/pallas_call | solution.py:331
  16.4 0.0 copy-start.3
  16.4 9.0 %all_to_all.10 = bf16[4,192,256]{2,1,0:T(8,128)(2,1)S(1)} all-to-all(bf16[4,192,256]{2,1,0:T(8,128)(2,1)S(1)} %bitcast.10), channel_id=1, replica_groups={{0,2,4,6},{8,10,12,14},{1,3,5,7},{9,11,13,15},{16,18,20,22},{24,26,28,3..., dimensions={0} | all-to-all | bytes 786432 | tf_op jit(solution)/shard_map/all_to_all | solution.py:249
  25.5 4.0 %collective-permute-start.2 = (bf16[192,256]{1,0:T(8,128)(2,1)S(1)}, bf16[192,256]{1,0:T(8,128)(2,1)S(1)}, u32[]{:S(2)}, u32[]{:S(2)}) collective-permute-start(bf16[192,256]{1,0:T(8,128)(2,1)S(1)} %convert_element_type.13), channel_id=1, source_target_pairs={{0,8},{2,10},{4,12},{6,14},{8,0},{10,2},{12,4},{14,6},{1,9},{3,11}... | collective-permute-start | bytes 294920 | tf_op jit(solution)/shard_map/ppermute | solution.py:260
  29.5 3.5 %collective-permute-done.2 = bf16[192,256]{1,0:T(8,128)(2,1)S(1)} collective-permute-done((bf16[192,256]{1,0:T(8,128)(2,1)S(1)}, bf16[192,256]{1,0:T(8,128)(2,1)S(1)}, u32[]{:S(2)}, u32[]{:S(2)}) %collective-permute-start.2) | collective-permute-done | bytes 98336 | tf_op jit(solution)/shard_map/ppermute | solution.py:260
  33.0 0.0 copy-start.2
  33.1 0.8 %broadcast_in_dim.4 = bf16[4,192,256]{2,1,0:T(8,128)(2,1)} broadcast(bf16[192,256]{1,0:T(8,128)(2,1)S(1)} %add_convert_fusion), dimensions={1,2} | broadcast | bytes 491520 | tf_op jit(solution)/shard_map/broadcast_in_dim | solution.py:263
  33.8 3.5 %all-to-all-start.1 = ((bf16[4,192,256]{2,1,0:T(8,128)(2,1)}), bf16[4,192,256]{2,1,0:T(8,128)(2,1)S(1)}, u32[]{:S(2)}, u32[]{:S(2)}) async-start(bf16[4,192,256]{2,1,0:T(8,128)(2,1)} %broadcast_in_dim.4), calls=%async_computation.1 | async-start | bytes 786432 | tf_op jit(solution)/shard_map/all_to_all | solution.py:264
  37.3 0.0 copy-done.3
  37.3 0.1 collective-permute-start.3
  37.4 1.9 %collective-permute-done.3.p_ref = bf16[2,128,1024]{2,1,0:T(8,128)(2,1)S(1)} collective-permute-done((bf16[2,128,1024]{2,1,0:T(8,128)(2,1)S(1)}, bf16[2,128,1024]{2,1,0:T(8,128)(2,1)S(1)}, u32[]{:S(2)}, u32[]{:S(2)}) %collective-permute-start.3) | collective-permute-done | bytes 524320 | tf_op jit(solution)/shard_map/ppermute | solution.py:296
  39.3 1.0 %shard_map.50 = (bf16[1024,256]{1,0:T(8,128)(2,1)S(1)}, bf16[1024,256]{1,0:T(8,128)(2,1)S(1)}, bf16[512,512]{1,0:T(8,128)(2,1)S(1)}) custom-call(bf16[2,128,1024]{2,1,0:T(8,128)(2,1)S(1)} %collective-permute-done.3.p_ref), custom_call_target="tpu_custom_call" | custom-call | flops 500000000 | bytes 2000000 | tf_op jit(solution)/shard_map/pallas_call | solution.py:308
  40.3 2.9 %all-to-all-done.1 = bf16[4,192,256]{2,1,0:T(8,128)(2,1)S(1)} async-done(((bf16[4,192,256]{2,1,0:T(8,128)(2,1)}), bf16[4,192,256]{2,1,0:T(8,128)(2,1)S(1)}, u32[]{:S(2)}, u32[]{:S(2)}) %all-to-all-start.1) | async-done | bytes 393248 | tf_op jit(solution)/shard_map/all_to_all | solution.py:264
  43.1 0.0 copy-done.2
  43.1 3.2 %shard_map.51 = bf16[3,2,128,1024]{3,2,1,0:T(8,128)(2,1)} custom-call(s32[3]{0:T(128)S(1)} %copy-done.2, bf16[768,256]{1,0:T(8,128)(2,1)S(1)} %bitcast.13, bf16[1024,256]{1,0:T(8,128)(2,1)S(1)} %get-tuple-element.12.minus_ref, bf16[1024,256]{1,0:T(8,128)(2,1)S(1)} %get-tuple-element.13.plus_ref, bf16[512,512]{1,0:T(8,128)(2,1)S(1)} %get-tuple-element.14.s_ref), custom_call_target="tpu_custom_call" | custom-call | flops 2400000000 | bytes 3000000 | tf_op jit(solution)/shard_map/pallas_call | solution.py:228
  (5 shorter events, 0.1 us)
Async XLA Ops:
  1.2 11.7 %collective-permute-start = (bf16[696,256]{1,0:T(8,128)(2,1)S(1)}, bf16[696,256]{1,0:T(8,128)(2,1)S(1)}, u32[]{:S(2)}, u32[]{:S(2)}) collective-permute-start(bf16[696,256]{1,0:T(8,128)(2,1)S(1)} %get-tuple-element.10), channel_id=1, source_target_pairs={{0,2},{2,0},{4,6},{6,4},{8,10},{10,8},{12,14},{14,12},{1,3},{3,1},... | collective-permute-start | bytes 1069064 | tf_op jit(solution)/shard_map/ppermute | solution.py:290
  4.3 10.9 %collective-permute-start.1 = (bf16[696,256]{1,0:T(8,128)(2,1)S(1)}, bf16[696,256]{1,0:T(8,128)(2,1)S(1)}, u32[]{:S(2)}, u32[]{:S(2)}) collective-permute-start(bf16[696,256]{1,0:T(8,128)(2,1)S(1)} %get-tuple-element.11.own_ref), channel_id=1, source_target_pairs={{4,0},{14,2},{8,4},{2,6},{12,8},{6,10},{0,12},{10,14},{5,1},{15,3}... | collective-permute-start | bytes 1069064 | tf_op jit(solution)/shard_map/ppermute | solution.py:291
  7.9 1.1 %copy-start = (bf16[1,2,256,3,216]{2,4,3,1,0:T(8,128)(2,1)S(1)}, bf16[1,2,256,3,216]{2,4,3,1,0:T(8,128)(2,1)}, u32[]{:S(2)}) copy-start(bf16[1,2,256,3,216]{2,4,3,1,0:T(8,128)(2,1)} %param.4) | copy-start | bytes 1990660
  9.0 0.7 %copy-start.1 = (bf16[1,3,3,3,2,216]{5,4,3,2,1,0:T(2,128)(2,1)S(1)}, bf16[1,3,3,3,2,216]{5,4,3,2,1,0:T(2,128)(2,1)}, u32[]{:S(2)}) copy-start(bf16[1,3,3,3,2,216]{5,4,3,2,1,0:T(2,128)(2,1)} %param.5) | copy-start | bytes 69988
  16.4 20.9 %copy-start.3 = (bf16[1,2,128,1024]{3,2,1,0:T(8,128)(2,1)S(1)}, bf16[1,2,128,1024]{3,2,1,0:T(8,128)(2,1)}, u32[]{:S(2)}) copy-start(bf16[1,2,128,1024]{3,2,1,0:T(8,128)(2,1)} %param.7) | copy-start | bytes 1572868
  25.5 7.5 %collective-permute-start.2 = (bf16[192,256]{1,0:T(8,128)(2,1)S(1)}, bf16[192,256]{1,0:T(8,128)(2,1)S(1)}, u32[]{:S(2)}, u32[]{:S(2)}) collective-permute-start(bf16[192,256]{1,0:T(8,128)(2,1)S(1)} %convert_element_type.13), channel_id=1, source_target_pairs={{0,8},{2,10},{4,12},{6,14},{8,0},{10,2},{12,4},{14,6},{1,9},{3,11}... | collective-permute-start | bytes 294920 | tf_op jit(solution)/shard_map/ppermute | solution.py:260
  33.0 10.1 %copy-start.2 = (s32[3]{0:T(128)S(1)}, s32[3]{0:T(128)}, u32[]{:S(2)}) copy-start(s32[3]{0:T(128)} %dirs_ref.1) | copy-start | bytes 40
  33.8 9.3 %all-to-all-start.1 = ((bf16[4,192,256]{2,1,0:T(8,128)(2,1)}), bf16[4,192,256]{2,1,0:T(8,128)(2,1)S(1)}, u32[]{:S(2)}, u32[]{:S(2)}) async-start(bf16[4,192,256]{2,1,0:T(8,128)(2,1)} %broadcast_in_dim.4), calls=%async_computation.1 | async-start | bytes 786432 | tf_op jit(solution)/shard_map/all_to_all | solution.py:264
  37.3 2.0 %collective-permute-start.3 = (bf16[2,128,1024]{2,1,0:T(8,128)(2,1)S(1)}, bf16[2,128,1024]{2,1,0:T(8,128)(2,1)S(1)}, u32[]{:S(2)}, u32[]{:S(2)}) collective-permute-start(bf16[2,128,1024]{2,1,0:T(8,128)(2,1)S(1)} %bitcast.16), channel_id=1, source_target_pairs={{1,0},{0,1},{3,2},{2,3},{5,4},{4,5},{7,6},{6,7},{9,8},{8,9},{11,10... | collective-permute-start | bytes 1572872 | tf_op jit(solution)/shard_map/ppermute | solution.py:296

commit v5 on v4

--- a/solution.py
+++ b/solution.py
@@ -127,31 +127,32 @@
         o_ref[pl.ds(index * vectors, vectors), :] = packed.astype(BF16)
 
 
-def pair_product(half, left_ref, right_ref, w_ref):
-    even = lax.rem(lax.axis_index("space"), 2) == 0
-    left, right = left_ref[...], right_ref[...]
-    field = jnp.where(even, left, right)
-    ahead = jnp.where(even, right, left)
+def rotated(half, field, w_ref):
     columns = dot(identity(half), field[6 * half :, :half], 1, 1)
     vec = [field[comp * half : (comp + 1) * half, :].astype(F32) for comp in range(6)]
     for comp, value in enumerate(adjoint_product(columns, 0, vec)):
-        w_ref[pl.ds(comp * half, half), :] = value
-    return packed_elemental(
-        w_ref[pl.ds(0, 3 * half), :].astype(BF16),
-        w_ref[pl.ds(3 * half, 3 * half), :].astype(BF16),
-        ahead[: 3 * half],
-        ahead[3 * half : 6 * half],
-    )
-
-
-def first_pair_kernel(half, own_ref, across_ref, o_ref, w_ref):
-    o_ref[...] = pair_product(half, own_ref, across_ref, w_ref)
-
-
-def second_pair_kernel(half, across_ref, along_ref, flat_ref, first_ref, o_ref, w_ref):
+        w_ref[pl.ds(comp * half, half), :] = value.astype(w_ref.dtype)
+
+
+def early_kernel(half, own_ref, along_ref, w_ref):
+    even = lax.rem(lax.axis_index("space"), 2) == 0
+    rotated(half, jnp.where(even, own_ref[...], along_ref[...]), w_ref)
+
+
+def late_kernel(half, early_ref, own_ref, across_ref, along_ref, flat_ref, o_ref, w_ref):
     done = flat_ref.shape[0]
     o_ref[pl.ds(0, done), :] = flat_ref[...]
-    packed = first_ref[...] + pair_product(half, across_ref, along_ref, w_ref)
+    even = lax.rem(lax.axis_index("space"), 2) == 0
+    rotated(half, across_ref[...], w_ref)
+    real, imag = pl.ds(0, 3 * half), pl.ds(3 * half, 3 * half)
+    packed = packed_elemental(
+        early_ref[real, :], early_ref[imag, :], across_ref[real, :], across_ref[imag, :]
+    ) + packed_elemental(
+        w_ref[real, :].astype(BF16),
+        w_ref[imag, :].astype(BF16),
+        jnp.where(even, along_ref[real, :], own_ref[real, :]),
+        jnp.where(even, along_ref[imag, :], own_ref[imag, :]),
+    )
     o_ref[pl.ds(done, packed.shape[0]), :] = packed.astype(BF16)
 
 
@@ -317,26 +318,27 @@
         cost_estimate=pl.CostEstimate(flops=500_000_000, bytes_accessed=2_000_000, transcendentals=0),
         compiler_params=PARAMS,
     )(partner)
-    pair_cost = pl.CostEstimate(flops=200_000_000, bytes_accessed=2_000_000, transcendentals=0)
-    pair_scratch = [pltpu.VMEM((6 * half, vectors), F32)]
-    upright = pl.pallas_call(
-        functools.partial(first_pair_kernel, half),
-        out_shape=jax.ShapeDtypeStruct((vectors, vectors), F32),
+    early = pl.pallas_call(
+        functools.partial(early_kernel, half),
+        out_shape=jax.ShapeDtypeStruct((6 * half, vectors), BF16),
         in_specs=[VMEM] * 2,
         out_specs=VMEM,
-        scratch_shapes=pair_scratch,
-        cost_estimate=pair_cost,
-        compiler_params=PARAMS,
-    )(along, from_across)
+        cost_estimate=pl.CostEstimate(
+            flops=20_000_000, bytes_accessed=1_000_000, transcendentals=0
+        ),
+        compiler_params=PARAMS,
+    )(along, from_along)
     packed = pl.pallas_call(
-        functools.partial(second_pair_kernel, half),
+        functools.partial(late_kernel, half),
         out_shape=jax.ShapeDtypeStruct((3 * vectors, vectors), BF16),
-        in_specs=[VMEM] * 4,
+        in_specs=[VMEM] * 5,
         out_specs=VMEM,
-        scratch_shapes=pair_scratch,
-        cost_estimate=pair_cost,
-        compiler_params=PARAMS,
-    )(from_across, from_along, flat, upright)
+        scratch_shapes=[pltpu.VMEM((6 * half, vectors), F32)],
+        cost_estimate=pl.CostEstimate(
+            flops=400_000_000, bytes_accessed=2_000_000, transcendentals=0
+        ),
+        compiler_params=PARAMS,
+    )(early, along, from_across, from_along, flat)
     packed = sum_over_space(packed, ranks)
     shape = (dirs.shape[0], 2, columns, SPIN * vectors)
     result = last_call(dirs, packed, minus, plus, table, shape)

time: 46.7 us -> 46.8 us (level)
  waiting for transfers between devices: 9.3 us -> 13.6 us
  starting transfers between devices: 14.2 us -> 10.6 us
  Pallas kernels: 11 us -> 10.4 us
    ppermute x1, starting transfers between devices: 3.03 us -> 0.01 us  [blocks(): lax.ppermute(across, 'space', [(i, i ^ 1) for i in range(ranks)])]
    ppermute x1, starting transfers between devices: 4.04 us -> 1.97 us  [sum_over_space(): lax.ppermute(total.astype(BF16), 'space', [(i, i ^ stride) for i in range...]
    ppermute x1, waiting for transfers between devices: 0.01 us -> 1.62 us  [blocks(): lax.ppermute(across, 'space', [(i, i ^ 1) for i in range(ranks)])]
    ppermute x1, starting transfers between devices: 3.6 us -> 5.13 us  [blocks(): lax.ppermute(along, 'space', [((i + 2) % ranks if i % 2 == 0 else (i - 2)...]
    ppermute x1, waiting for transfers between devices: 1.05 us -> 2.55 us  [blocks(): lax.ppermute(along, 'space', [((i + 2) % ranks if i % 2 == 0 else (i - 2)...]
    ppermute x1, waiting for transfers between devices: 3.47 us -> 4.66 us  [sum_over_space(): lax.ppermute(total.astype(BF16), 'space', [(i, i ^ stride) for i in range...]
    pallas_call x2, Pallas kernels: 2.42 us -> 1.81 us  [the longest x1 1.24 us: blocks(): pl.pallas_call(functools.partial(late_kernel, half), out_shape=jax.ShapeD...]
  transfers between devices with their start and end apart: 5 -> 5, of which waited for: 4 -> 5; matrix products, arithmetic and copies ran while one was open for 0% -> 0% of each run, Pallas kernels for 12% -> 10%
where the time goes in v5:
time: 46.8 us; the launch traced here: 46.4 us
  waiting for transfers between devices  13.6 us (29%)
  starting transfers between devices  10.6 us (23%)
  Pallas kernels  10.4 us (22%)
  blocking collectives  8.95 us (19%)
  local copies, waits for them, and re-layouts  2.62 us (6%)
    all_to_all x1, blocking collectives, sum_over_space(): lax.all_to_all(partial.reshape(near, rows // near, width), 'space', 0, 0,...  8.95 us
    ppermute x1, starting transfers between devices, blocks(): lax.ppermute(along, 'space', [((i + 2) % ranks if i % 2 == 0 else (i - 2)...  5.13 us
    ppermute x1, waiting for transfers between devices, sum_over_space(): lax.ppermute(total.astype(BF16), 'space', [(i, i ^ stride) for i in range...  4.66 us
    all_to_all x1, starting transfers between devices, sum_over_space(): lax.all_to_all(whole, 'space', 0, 0, axis_index_groups=groups, tiled=True)  3.46 us
    pallas_call x1, Pallas kernels, blocks(): pl.pallas_call(functools.partial(front_kernel, sites), out_shape=jax.Shap...  3.18 us
    pallas_call x1, Pallas kernels, last_call(): pl.pallas_call(last_kernel, in_specs=[pl.BlockSpec(memory_space=pltpu.SME...  3.17 us
    all_to_all x1, waiting for transfers between devices, sum_over_space(): lax.all_to_all(whole, 'space', 0, 0, axis_index_groups=groups, tiled=True)  2.87 us
    ppermute x1, waiting for transfers between devices, blocks(): lax.ppermute(along, 'space', [((i + 2) % ranks if i % 2 == 0 else (i - 2)...  2.55 us
  transfers between devices with their start and end apart: 5, of which 5 were waited for; matrix products, arithmetic and copies ran while one was open for 0% of the time, Pallas kernels for 10%

profile of v5, /device:TPU:0, one launch (start us, length us, event | category | flops | bytes accessed | tf_op | source)
XLA Modules:
  0.0 46.4 jit_solution(3024262095902388881)
XLA Ops:
  0.0 1.2 %shard_map.46 = (bf16[696,256]{1,0:T(8,128)(2,1)S(1)}, bf16[696,256]{1,0:T(8,128)(2,1)S(1)}) custom-call(bf16[1296,256]{1,0:T(8,128)(2,1)} %bitcast.11, bf16[27,2,216]{2,1,0:T(2,128)(2,1)} %bitcast.14), custom_call_target="tpu_custom_call" | custom-call | tf_op jit(solution)/shard_map/pallas_call | solution.py:279
  1.2 5.1 %collective-permute-start = (bf16[696,256]{1,0:T(8,128)(2,1)S(1)}, bf16[696,256]{1,0:T(8,128)(2,1)S(1)}, u32[]{:S(2)}, u32[]{:S(2)}) collective-permute-start(bf16[696,256]{1,0:T(8,128)(2,1)S(1)} %get-tuple-element.10.own_ref), channel_id=1, source_target_pairs={{4,0},{14,2},{8,4},{2,6},{12,8},{6,10},{0,12},{10,14},{5,1},{15,3}... | collective-permute-start | bytes 1069064 | tf_op jit(solution)/shard_map/ppermute | solution.py:292
  6.4 0.0 collective-permute-start.1
  6.4 1.1 %copy-done = bf16[1,2,256,3,216]{2,4,3,1,0:T(8,128)(2,1)S(1)} copy-done((bf16[1,2,256,3,216]{2,4,3,1,0:T(8,128)(2,1)S(1)}, bf16[1,2,256,3,216]{2,4,3,1,0:T(8,128)(2,1)}, u32[]{:S(2)}) %copy-start) | copy-done | bytes 663576
  7.5 0.7 %copy-done.1 = bf16[1,3,3,3,2,216]{5,4,3,2,1,0:T(2,128)(2,1)S(1)} copy-done((bf16[1,3,3,3,2,216]{5,4,3,2,1,0:T(2,128)(2,1)S(1)}, bf16[1,3,3,3,2,216]{5,4,3,2,1,0:T(2,128)(2,1)}, u32[]{:S(2)}) %copy-start.1) | copy-done | bytes 23352
  8.2 3.2 %shard_map.48.flat_ref = bf16[512,256]{1,0:T(8,128)(2,1)S(1)} custom-call(bf16[1296,256]{1,0:T(8,128)(2,1)S(1)} %bitcast.12, bf16[27,2,216]{2,1,0:T(2,128)(2,1)S(1)} %bitcast.15), custom_call_target="tpu_custom_call" | custom-call | flops 700000000 | bytes 8000000 | tf_op jit(solution)/shard_map/pallas_call | solution.py:299
  11.4 2.6 %collective-permute-done.along_ref = bf16[696,256]{1,0:T(8,128)(2,1)S(1)} collective-permute-done((bf16[696,256]{1,0:T(8,128)(2,1)S(1)}, bf16[696,256]{1,0:T(8,128)(2,1)S(1)}, u32[]{:S(2)}, u32[]{:S(2)}) %collective-permute-start) | collective-permute-done | bytes 356384 | tf_op jit(solution)/shard_map/ppermute | solution.py:292
  14.0 0.6 %shard_map.47.early_ref = bf16[672,256]{1,0:T(8,128)(2,1)S(1)} custom-call(bf16[696,256]{1,0:T(8,128)(2,1)S(1)} %get-tuple-element.10.own_ref, bf16[696,256]{1,0:T(8,128)(2,1)S(1)} %collective-permute-done.along_ref), custom_call_target="tpu_custom_call" | custom-call | flops 20000000 | bytes 1000000 | tf_op jit(solution)/shard_map/pallas_call | solution.py:321
  14.5 1.6 %collective-permute-done.1.across_ref = bf16[696,256]{1,0:T(8,128)(2,1)S(1)} collective-permute-done((bf16[696,256]{1,0:T(8,128)(2,1)S(1)}, bf16[696,256]{1,0:T(8,128)(2,1)S(1)}, u32[]{:S(2)}, u32[]{:S(2)}) %collective-permute-start.1) | collective-permute-done | bytes 356384 | tf_op jit(solution)/shard_map/ppermute | solution.py:291
  16.2 1.2 %shard_map.49 = bf16[768,256]{1,0:T(8,128)(2,1)S(1)} custom-call(bf16[672,256]{1,0:T(8,128)(2,1)S(1)} %shard_map.47.early_ref, bf16[696,256]{1,0:T(8,128)(2,1)S(1)} %get-tuple-element.10.own_ref, bf16[696,256]{1,0:T(8,128)(2,1)S(1)} %collective-permute-done.1.across_ref, bf16[696,256]{1,0:T(8,128)(2,1)S(1)} %collective-permute-done.along_ref, ...), custom_call_target="tpu_custom_call" | custom-call | flops 400000000 | bytes 2000000 | tf_op jit(solution)/shard_map/pallas_call | solution.py:331
  17.4 0.0 copy-start.3
  17.4 9.0 %all_to_all.10 = bf16[4,192,256]{2,1,0:T(8,128)(2,1)S(1)} all-to-all(bf16[4,192,256]{2,1,0:T(8,128)(2,1)S(1)} %bitcast.10), channel_id=1, replica_groups={{0,2,4,6},{8,10,12,14},{1,3,5,7},{9,11,13,15},{16,18,20,22},{24,26,28,3..., dimensions={0} | all-to-all | bytes 786432 | tf_op jit(solution)/shard_map/all_to_all | solution.py:250
  26.4 2.0 %collective-permute-start.2 = (bf16[192,256]{1,0:T(8,128)(2,1)S(1)}, bf16[192,256]{1,0:T(8,128)(2,1)S(1)}, u32[]{:S(2)}, u32[]{:S(2)}) collective-permute-start(bf16[192,256]{1,0:T(8,128)(2,1)S(1)} %convert_element_type.13), channel_id=1, source_target_pairs={{0,8},{2,10},{4,12},{6,14},{8,0},{10,2},{12,4},{14,6},{1,9},{3,11}... | collective-permute-start | bytes 294920 | tf_op jit(solution)/shard_map/ppermute | solution.py:261
  28.4 4.7 %collective-permute-done.2 = bf16[192,256]{1,0:T(8,128)(2,1)S(1)} collective-permute-done((bf16[192,256]{1,0:T(8,128)(2,1)S(1)}, bf16[192,256]{1,0:T(8,128)(2,1)S(1)}, u32[]{:S(2)}, u32[]{:S(2)}) %collective-permute-start.2) | collective-permute-done | bytes 98336 | tf_op jit(solution)/shard_map/ppermute | solution.py:261
  33.1 0.0 copy-start.2
  33.1 0.8 %broadcast_in_dim.4 = bf16[4,192,256]{2,1,0:T(8,128)(2,1)} broadcast(bf16[192,256]{1,0:T(8,128)(2,1)S(1)} %add_convert_fusion), dimensions={1,2} | broadcast | bytes 491520 | tf_op jit(solution)/shard_map/broadcast_in_dim | solution.py:264
  33.9 3.5 %all-to-all-start.1 = ((bf16[4,192,256]{2,1,0:T(8,128)(2,1)}), bf16[4,192,256]{2,1,0:T(8,128)(2,1)S(1)}, u32[]{:S(2)}, u32[]{:S(2)}) async-start(bf16[4,192,256]{2,1,0:T(8,128)(2,1)} %broadcast_in_dim.4), calls=%async_computation.1 | async-start | bytes 786432 | tf_op jit(solution)/shard_map/all_to_all | solution.py:265
  37.4 0.0 copy-done.3
  37.4 0.1 collective-permute-start.3
  37.4 1.9 %collective-permute-done.3.p_ref = bf16[2,128,1024]{2,1,0:T(8,128)(2,1)S(1)} collective-permute-done((bf16[2,128,1024]{2,1,0:T(8,128)(2,1)S(1)}, bf16[2,128,1024]{2,1,0:T(8,128)(2,1)S(1)}, u32[]{:S(2)}, u32[]{:S(2)}) %collective-permute-start.3) | collective-permute-done | bytes 524320 | tf_op jit(solution)/shard_map/ppermute | solution.py:297
  39.3 1.0 %shard_map.50 = (bf16[1024,256]{1,0:T(8,128)(2,1)S(1)}, bf16[1024,256]{1,0:T(8,128)(2,1)S(1)}, bf16[512,512]{1,0:T(8,128)(2,1)S(1)}) custom-call(bf16[2,128,1024]{2,1,0:T(8,128)(2,1)S(1)} %collective-permute-done.3.p_ref), custom_call_target="tpu_custom_call" | custom-call | flops 500000000 | bytes 2000000 | tf_op jit(solution)/shard_map/pallas_call | solution.py:309
  40.3 2.9 %all-to-all-done.1 = bf16[4,192,256]{2,1,0:T(8,128)(2,1)S(1)} async-done(((bf16[4,192,256]{2,1,0:T(8,128)(2,1)}), bf16[4,192,256]{2,1,0:T(8,128)(2,1)S(1)}, u32[]{:S(2)}, u32[]{:S(2)}) %all-to-all-start.1) | async-done | bytes 393248 | tf_op jit(solution)/shard_map/all_to_all | solution.py:265
  43.2 0.0 copy-done.2
  43.2 3.2 %shard_map.51 = bf16[3,2,128,1024]{3,2,1,0:T(8,128)(2,1)} custom-call(s32[3]{0:T(128)S(1)} %copy-done.2, bf16[768,256]{1,0:T(8,128)(2,1)S(1)} %bitcast.13, bf16[1024,256]{1,0:T(8,128)(2,1)S(1)} %get-tuple-element.12.minus_ref, bf16[1024,256]{1,0:T(8,128)(2,1)S(1)} %get-tuple-element.13.plus_ref, bf16[512,512]{1,0:T(8,128)(2,1)S(1)} %get-tuple-element.14.s_ref), custom_call_target="tpu_custom_call" | custom-call | flops 2400000000 | bytes 3000000 | tf_op jit(solution)/shard_map/pallas_call | solution.py:229
  (5 shorter events, 0.1 us)
Async XLA Ops:
  1.2 12.7 %collective-permute-start = (bf16[696,256]{1,0:T(8,128)(2,1)S(1)}, bf16[696,256]{1,0:T(8,128)(2,1)S(1)}, u32[]{:S(2)}, u32[]{:S(2)}) collective-permute-start(bf16[696,256]{1,0:T(8,128)(2,1)S(1)} %get-tuple-element.10.own_ref), channel_id=1, source_target_pairs={{4,0},{14,2},{8,4},{2,6},{12,8},{6,10},{0,12},{10,14},{5,1},{15,3}... | collective-permute-start | bytes 1069064 | tf_op jit(solution)/shard_map/ppermute | solution.py:292
  6.4 9.8 %collective-permute-start.1 = (bf16[696,256]{1,0:T(8,128)(2,1)S(1)}, bf16[696,256]{1,0:T(8,128)(2,1)S(1)}, u32[]{:S(2)}, u32[]{:S(2)}) collective-permute-start(bf16[696,256]{1,0:T(8,128)(2,1)S(1)} %get-tuple-element.11), channel_id=1, source_target_pairs={{0,2},{2,0},{4,6},{6,4},{8,10},{10,8},{12,14},{14,12},{1,3},{3,1},... | collective-permute-start | bytes 1069064 | tf_op jit(solution)/shard_map/ppermute | solution.py:291
  6.4 1.1 %copy-start = (bf16[1,2,256,3,216]{2,4,3,1,0:T(8,128)(2,1)S(1)}, bf16[1,2,256,3,216]{2,4,3,1,0:T(8,128)(2,1)}, u32[]{:S(2)}) copy-start(bf16[1,2,256,3,216]{2,4,3,1,0:T(8,128)(2,1)} %param.4) | copy-start | bytes 1990660
  7.5 0.7 %copy-start.1 = (bf16[1,3,3,3,2,216]{5,4,3,2,1,0:T(2,128)(2,1)S(1)}, bf16[1,3,3,3,2,216]{5,4,3,2,1,0:T(2,128)(2,1)}, u32[]{:S(2)}) copy-start(bf16[1,3,3,3,2,216]{5,4,3,2,1,0:T(2,128)(2,1)} %param.5) | copy-start | bytes 69988
  17.4 19.9 %copy-start.3 = (bf16[1,2,128,1024]{3,2,1,0:T(8,128)(2,1)S(1)}, bf16[1,2,128,1024]{3,2,1,0:T(8,128)(2,1)}, u32[]{:S(2)}) copy-start(bf16[1,2,128,1024]{3,2,1,0:T(8,128)(2,1)} %param.7) | copy-start | bytes 1572868
  26.4 6.6 %collective-permute-start.2 = (bf16[192,256]{1,0:T(8,128)(2,1)S(1)}, bf16[192,256]{1,0:T(8,128)(2,1)S(1)}, u32[]{:S(2)}, u32[]{:S(2)}) collective-permute-start(bf16[192,256]{1,0:T(8,128)(2,1)S(1)} %convert_element_type.13), channel_id=1, source_target_pairs={{0,8},{2,10},{4,12},{6,14},{8,0},{10,2},{12,4},{14,6},{1,9},{3,11}... | collective-permute-start | bytes 294920 | tf_op jit(solution)/shard_map/ppermute | solution.py:261
  33.1 10.1 %copy-start.2 = (s32[3]{0:T(128)S(1)}, s32[3]{0:T(128)}, u32[]{:S(2)}) copy-start(s32[3]{0:T(128)} %dirs_ref.1) | copy-start | bytes 40
  33.9 9.3 %all-to-all-start.1 = ((bf16[4,192,256]{2,1,0:T(8,128)(2,1)}), bf16[4,192,256]{2,1,0:T(8,128)(2,1)S(1)}, u32[]{:S(2)}, u32[]{:S(2)}) async-start(bf16[4,192,256]{2,1,0:T(8,128)(2,1)} %broadcast_in_dim.4), calls=%async_computation.1 | async-start | bytes 786432 | tf_op jit(solution)/shard_map/all_to_all | solution.py:265
  37.4 2.0 %collective-permute-start.3 = (bf16[2,128,1024]{2,1,0:T(8,128)(2,1)S(1)}, bf16[2,128,1024]{2,1,0:T(8,128)(2,1)S(1)}, u32[]{:S(2)}, u32[]{:S(2)}) collective-permute-start(bf16[2,128,1024]{2,1,0:T(8,128)(2,1)S(1)} %bitcast.16), channel_id=1, source_target_pairs={{1,0},{0,1},{3,2},{2,3},{5,4},{4,5},{7,6},{6,7},{9,8},{8,9},{11,10... | collective-permute-start | bytes 1572872 | tf_op jit(solution)/shard_map/ppermute | solution.py:297
